TPU v7x, 128 devices: a whole 4x4x4 slice. The times are simulated.
128 devices in a mesh: section: 4 (over x_hi, core), dp: 32 (over y, z, x_lo).
Axes of the slice: x: 4 (x_hi: 2, x_lo: 2; x = x_hi * 2 + x_lo), y: 4, z: 4, core: 2. Of those that a mesh axis runs over, the one named last changes fastest.
Arguments:
- inputs: bfloat16 [2, 32, 128, 1024], P(None, 'dp'), may hold values from -6 to 6
- cotangent: bfloat16 [2, 32, 128, 1024], P(None, 'dp'), may hold values from -6 to 6
- lengths: int32 [2, 32], P(None, 'dp'), may hold values from 32 to 128, as said below
- attn_gain: float32 [4096], P(('section', 'dp')), may hold values from 0.25 to 1.75
- w_query: float32 [4096, 1024], P(('section', 'dp')), may hold values from -0.1875 to 0.1875
- w_key: float32 [4096, 128], P(('section', 'dp')), may hold values from -0.1875 to 0.1875
- w_value: float32 [4096, 128], P(('section', 'dp')), may hold values from -0.1875 to 0.1875
- w_out: float32 [4096, 1024], P(('section', 'dp')), may hold values from -0.75 to 0.75
- ffn_gain: float32 [4096], P(('section', 'dp')), may hold values from 0.25 to 1.75
- w_up: float32 [4096, 4096], P(('section', 'dp')), may hold values from -0.1875 to 0.1875
- w_down: float32 [16384, 1024], P(('section', 'dp')), may hold values from -0.09375 to 0.09375
Outputs:
- final: bfloat16 [2, 32, 128, 1024], P(None, 'dp', 'section')
- input_grad: bfloat16 [2, 32, 128, 1024], P(None, 'dp', 'section')
- grad_attn_gain: float32 [4096], P(('section', 'dp'))
- grad_query: float32 [4096, 1024], P(('section', 'dp'))
- grad_key: float32 [4096, 128], P(('section', 'dp'))
- grad_value: float32 [4096, 128], P(('section', 'dp'))
- grad_out: float32 [4096, 1024], P(('section', 'dp'))
- grad_ffn_gain: float32 [4096], P(('section', 'dp'))
- grad_up: float32 [4096, 4096], P(('section', 'dp'))
- grad_down: float32 [16384, 1024], P(('section', 'dp'))
Inputs may be any that keep to these rules, and one draw needn't show every extreme that they name: `lengths`: some sequence is exactly 128 tokens long.
All inputs are finite; a program needn't handle non-finite values.
Results may differ from a plain program's by a relative error of at most 0.035.
Values may be sent and summed in bfloat16 or wider, within the bound.
A program may use at most 832 MiB of HBM per device.

v0:
```python
import jax
import jax.numpy as jnp
from jax import lax
from jax.sharding import PartitionSpec as P

D = 1024
HEADS = 8
HD = 128
FF = 4096


NORM_EPS = 1e-06
NEG_FILL = -1000000000.0


def shifted(block, axis, distance):
    devices = range(lax.axis_size(axis))
    route = [(i - distance, i) for i in devices if i - distance in devices]
    return lax.ppermute(block, axis, route)


def plain_dot(left_side, right_side):
    return jnp.dot(left_side, right_side, preferred_element_type=jnp.float32)


def contract_rows(left_side, right_side):
    return lax.dot_general(
        left_side, right_side, (((0,), (0,)), ((), ())), preferred_element_type=jnp.float32
    )


def times_transpose(left_side, right_side):
    return lax.dot_general(
        left_side, right_side, (((1,), (1,)), ((), ())), preferred_element_type=jnp.float32
    )


def rms_parts(values):
    factor = lax.rsqrt(jnp.mean(values * values, axis=-1, keepdims=True) + NORM_EPS)
    return (values * factor, factor)


def norm_back(grad_normed, normed, factor):
    return factor * (grad_normed - normed * jnp.mean(grad_normed * normed, axis=-1, keepdims=True))


def kept_zeros(seq_len):
    single = jnp.float32
    half = jnp.bfloat16
    return (
        jnp.zeros((seq_len, 1), single),
        jnp.zeros((seq_len, D), single),
        jnp.zeros((seq_len, 1), single),
        jnp.zeros((seq_len, D), half),
        jnp.zeros((seq_len, HEADS, HD), half),
        jnp.zeros((seq_len, HD), half),
        jnp.zeros((seq_len, HD), half),
        jnp.zeros((HEADS, seq_len, seq_len), single),
        jnp.zeros((HEADS, seq_len, seq_len), half),
        jnp.zeros((seq_len, D), half),
        jnp.zeros((seq_len, D), single),
        jnp.zeros((seq_len, 1), single),
        jnp.zeros((seq_len, D), half),
        jnp.zeros((seq_len, FF), single),
        jnp.zeros((seq_len, FF), half),
    )


def layer_forward(hidden_in, length, params):
    attn_gain, w_query, w_key, w_value, w_out, ffn_gain, w_up, w_down = params
    hidden = hidden_in.astype(jnp.float32)
    seq_len = hidden.shape[0]
    positions = jnp.arange(seq_len)
    pad_mask = (positions < length).astype(jnp.float32)[:, None]
    normed_a, factor_a = rms_parts(hidden)
    attn_in = (normed_a * attn_gain.astype(jnp.float32)).astype(jnp.bfloat16)
    queries = plain_dot(attn_in, w_query).astype(jnp.bfloat16)
    keys_all = plain_dot(attn_in, w_key).astype(jnp.bfloat16)
    values_all = plain_dot(attn_in, w_value).astype(jnp.bfloat16)
    head_count = queries.shape[1] // HD
    query_heads = queries.reshape(seq_len, head_count, HD)
    allowed = (positions[None, :] <= positions[:, None]) & (positions[None, :] < length)
    scores = jnp.einsum(
        "thd,sd->hts", query_heads, keys_all, preferred_element_type=jnp.float32
    ) * HD ** (-0.5)
    scores = jnp.where(allowed[None], scores, NEG_FILL)
    row_max = jnp.max(scores, axis=-1, keepdims=True)
    exp_scores = jnp.exp(scores - row_max)
    attn_probs = exp_scores / jnp.sum(exp_scores, axis=-1, keepdims=True)
    probs_low = attn_probs.astype(jnp.bfloat16)
    mixed_heads = jnp.einsum(
        "hts,sd->thd", probs_low, values_all, preferred_element_type=jnp.float32
    )
    mixed_heads = mixed_heads.reshape(seq_len, head_count * HD).astype(jnp.bfloat16)
    after_attn = hidden + pad_mask * plain_dot(mixed_heads, w_out)
    normed_f, factor_f = rms_parts(after_attn)
    ffn_in = (normed_f * ffn_gain.astype(jnp.float32)).astype(jnp.bfloat16)
    pre_act = plain_dot(ffn_in, w_up)
    act_out = jax.nn.silu(pre_act).astype(jnp.bfloat16)
    result = (after_attn + pad_mask * plain_dot(act_out, w_down)).astype(jnp.bfloat16)
    kept_values = (
        pad_mask,
        normed_a,
        factor_a,
        attn_in,
        query_heads,
        keys_all,
        values_all,
        attn_probs,
        probs_low,
        mixed_heads,
        normed_f,
        factor_f,
        ffn_in,
        pre_act,
        act_out,
    )
    return (result, kept_values)


def layer_backward(kept_values, grad_in, params):
    attn_gain, w_query, w_key, w_value, w_out, ffn_gain, w_up, w_down = params
    (
        pad_mask,
        normed_a,
        factor_a,
        attn_in,
        query_heads,
        keys_all,
        values_all,
        attn_probs,
        probs_low,
        mixed_heads,
        normed_f,
        factor_f,
        ffn_in,
        pre_act,
        act_out,
    ) = kept_values
    seq_len = grad_in.shape[0]
    score_scale = HD ** (-0.5)
    grad_out = grad_in.astype(jnp.float32)
    grad_ffn = (grad_out * pad_mask).astype(jnp.bfloat16)
    g_down = contract_rows(act_out, grad_ffn)
    grad_act = times_transpose(grad_ffn, w_down)
    sigmoid_pre = jax.nn.sigmoid(pre_act)
    grad_pre = (grad_act * sigmoid_pre * (1.0 + pre_act * (1.0 - sigmoid_pre))).astype(jnp.bfloat16)
    g_up = contract_rows(ffn_in, grad_pre)
    grad_ffn_in = times_transpose(grad_pre, w_up)
    g_ffn_gain = jnp.sum(grad_ffn_in * normed_f, axis=0)
    grad_after = grad_out + norm_back(
        grad_ffn_in * ffn_gain.astype(jnp.float32), normed_f, factor_f
    )
    grad_attn = (grad_after * pad_mask).astype(jnp.bfloat16)
    g_out = contract_rows(mixed_heads, grad_attn)
    grad_mixed = times_transpose(grad_attn, w_out).astype(jnp.bfloat16)
    grad_mixed = grad_mixed.reshape(query_heads.shape)
    grad_probs = jnp.einsum(
        "thd,sd->hts", grad_mixed, values_all, preferred_element_type=jnp.float32
    )
    grad_values = jnp.einsum(
        "hts,thd->sd", probs_low, grad_mixed, preferred_element_type=jnp.float32
    ).astype(jnp.bfloat16)
    grad_scores = attn_probs * (
        grad_probs - jnp.sum(attn_probs * grad_probs, axis=-1, keepdims=True)
    )
    grad_scores = grad_scores.astype(jnp.bfloat16)
    grad_queries = (
        jnp.einsum("hts,sd->thd", grad_scores, keys_all, preferred_element_type=jnp.float32)
        * score_scale
    )
    grad_queries = grad_queries.reshape(seq_len, -1).astype(jnp.bfloat16)
    grad_keys = (
        jnp.einsum("hts,thd->sd", grad_scores, query_heads, preferred_element_type=jnp.float32)
        * score_scale
    ).astype(jnp.bfloat16)
    g_query = contract_rows(attn_in, grad_queries)
    g_key = contract_rows(attn_in, grad_keys)
    g_value = contract_rows(attn_in, grad_values)
    grad_attn_in = (
        times_transpose(grad_queries, w_query)
        + times_transpose(grad_keys, w_key)
        + times_transpose(grad_values, w_value)
    )
    g_attn_gain = jnp.sum(grad_attn_in * normed_a, axis=0)
    grad_hidden = grad_after + norm_back(
        grad_attn_in * attn_gain.astype(jnp.float32), normed_a, factor_a
    )
    return (
        grad_hidden.astype(jnp.bfloat16),
        (g_attn_gain, g_query, g_key, g_value, g_out, g_ffn_gain, g_up, g_down),
    )


def pick_length(lengths_here, micro_idx):
    slots = jnp.arange(lengths_here.shape[0])
    return jnp.sum(jnp.where(slots == micro_idx, lengths_here, 0))


def store_at(stack, fresh, micro_idx, writing):
    previous = lax.dynamic_index_in_dim(stack, micro_idx, 0, keepdims=False)
    return lax.dynamic_update_index_in_dim(stack, jnp.where(writing, fresh, previous), micro_idx, 0)


def body(
    inputs, cotangent, lengths, attn_gain, w_query, w_key, w_value, w_out, ffn_gain, w_up, w_down
):
    section_count = lax.axis_size("section")
    section_idx = lax.axis_index("section")
    micro_count = lengths.shape[0]
    lengths_here = lengths[:, 0]
    seq_len = inputs.shape[2]
    width = inputs.shape[3]
    own_inputs = inputs[:, 0]
    own_cotangent = cotangent[:, 0]
    layer_params = (
        lax.all_gather(attn_gain.astype(jnp.bfloat16), "dp", axis=0, tiled=True),
        lax.all_gather(w_query.astype(jnp.bfloat16), "dp", axis=0, tiled=True),
        lax.all_gather(w_key.astype(jnp.bfloat16), "dp", axis=0, tiled=True),
        lax.all_gather(w_value.astype(jnp.bfloat16), "dp", axis=0, tiled=True),
        lax.all_gather(w_out.astype(jnp.bfloat16), "dp", axis=0, tiled=True),
        lax.all_gather(ffn_gain.astype(jnp.bfloat16), "dp", axis=0, tiled=True),
        lax.all_gather(w_up.astype(jnp.bfloat16), "dp", axis=0, tiled=True),
        lax.all_gather(w_down.astype(jnp.bfloat16), "dp", axis=0, tiled=True),
    )
    layer_params = tuple(layer_params)
    tick_count = micro_count + section_count - 1
    carried = jnp.zeros((seq_len, width), jnp.bfloat16)
    final_full = jnp.zeros(own_inputs.shape, jnp.bfloat16)
    stash = tuple(
        (jnp.zeros((micro_count,) + blank.shape, blank.dtype) for blank in kept_zeros(seq_len))
    )
    for tick_idx in range(tick_count):
        micro_raw = tick_idx - section_idx
        active_now = (micro_raw >= 0) & (micro_raw < micro_count)
        micro_idx = jnp.clip(micro_raw, 0, micro_count - 1)
        fresh_input = lax.dynamic_index_in_dim(own_inputs, micro_idx, 0, keepdims=False)
        layer_in = jnp.where(section_idx == 0, fresh_input, carried)
        length = pick_length(lengths_here, micro_idx)

        def run_forward(operands):
            return layer_forward(operands[0], operands[1], layer_params)

        def skip_forward(operands):
            return (jnp.zeros_like(operands[0]), kept_zeros(seq_len))

        layer_out, kept_now = lax.cond(active_now, run_forward, skip_forward, (layer_in, length))
        stash = tuple(
            (store_at(stack, fresh, micro_idx, active_now) for stack, fresh in zip(stash, kept_now))
        )
        final_full = store_at(
            final_full, layer_out, micro_idx, active_now & (section_idx == section_count - 1)
        )
        if tick_idx + 1 < tick_count:
            carried = shifted(layer_out, "section", 1)
    layer_params = (
        lax.all_gather(attn_gain.astype(jnp.bfloat16), "dp", axis=0, tiled=True),
        lax.all_gather(w_query.astype(jnp.bfloat16), "dp", axis=0, tiled=True),
        lax.all_gather(w_key.astype(jnp.bfloat16), "dp", axis=0, tiled=True),
        lax.all_gather(w_value.astype(jnp.bfloat16), "dp", axis=0, tiled=True),
        lax.all_gather(w_out.astype(jnp.bfloat16), "dp", axis=0, tiled=True),
        lax.all_gather(ffn_gain.astype(jnp.bfloat16), "dp", axis=0, tiled=True),
        lax.all_gather(w_up.astype(jnp.bfloat16), "dp", axis=0, tiled=True),
        lax.all_gather(w_down.astype(jnp.bfloat16), "dp", axis=0, tiled=True),
    )
    layer_params = tuple(layer_params)
    grad_carried = jnp.zeros((seq_len, width), jnp.bfloat16)
    input_full = jnp.zeros(own_cotangent.shape, jnp.bfloat16)
    totals = tuple((jnp.zeros(weight.shape, jnp.float32) for weight in layer_params))
    for tick_idx in range(tick_count):
        micro_raw = tick_idx - (section_count - 1 - section_idx)
        active_now = (micro_raw >= 0) & (micro_raw < micro_count)
        micro_idx = jnp.clip(micro_raw, 0, micro_count - 1)
        fresh_grad = lax.dynamic_index_in_dim(own_cotangent, micro_idx, 0, keepdims=False)
        grad_in = jnp.where(section_idx == section_count - 1, fresh_grad, grad_carried)
        kept_now = tuple(
            (lax.dynamic_index_in_dim(stack, micro_idx, 0, keepdims=False) for stack in stash)
        )

        def run_backward(operands):
            return layer_backward(operands[0], operands[1], layer_params)

        def skip_backward(operands):
            return (
                jnp.zeros_like(operands[1]),
                tuple((jnp.zeros(weight.shape, jnp.float32) for weight in layer_params)),
            )

        grad_hidden, grad_terms = lax.cond(
            active_now, run_backward, skip_backward, (kept_now, grad_in)
        )
        totals = tuple((total + term for total, term in zip(totals, grad_terms)))
        input_full = store_at(input_full, grad_hidden, micro_idx, active_now & (section_idx == 0))
        if tick_idx + 1 < tick_count:
            grad_carried = shifted(grad_hidden, "section", -1)
    summed = (
        lax.psum_scatter(
            totals[0].astype(jnp.bfloat16), "dp", scatter_dimension=0, tiled=True
        ).astype(jnp.float32),
        lax.psum_scatter(
            totals[1].astype(jnp.bfloat16), "dp", scatter_dimension=0, tiled=True
        ).astype(jnp.float32),
        lax.psum_scatter(
            totals[2].astype(jnp.bfloat16), "dp", scatter_dimension=0, tiled=True
        ).astype(jnp.float32),
        lax.psum_scatter(
            totals[3].astype(jnp.bfloat16), "dp", scatter_dimension=0, tiled=True
        ).astype(jnp.float32),
        lax.psum_scatter(
            totals[4].astype(jnp.bfloat16), "dp", scatter_dimension=0, tiled=True
        ).astype(jnp.float32),
        lax.psum_scatter(
            totals[5].astype(jnp.bfloat16), "dp", scatter_dimension=0, tiled=True
        ).astype(jnp.float32),
        lax.psum_scatter(
            totals[6].astype(jnp.bfloat16), "dp", scatter_dimension=0, tiled=True
        ).astype(jnp.float32),
        lax.psum_scatter(
            totals[7].astype(jnp.bfloat16), "dp", scatter_dimension=0, tiled=True
        ).astype(jnp.float32),
    )
    received = (
        lax.all_to_all(final_full, "section", split_axis=1, concat_axis=0, tiled=True),
        lax.all_to_all(input_full, "section", split_axis=1, concat_axis=0, tiled=True),
    )
    row_part = seq_len // section_count
    final_rows = received[0].reshape(section_count, micro_count, row_part, width)[section_count - 1]
    input_rows = received[1].reshape(section_count, micro_count, row_part, width)[0]
    return (
        final_rows[:, None],
        input_rows[:, None],
        summed[0],
        summed[1],
        summed[2],
        summed[3],
        summed[4],
        summed[5],
        summed[6],
        summed[7],
    )


def solution(mesh):
    return jax.shard_map(
        body,
        mesh=mesh,
        in_specs=(
            P(None, "dp", None, None),
            P(None, "dp", None, None),
            P(None, "dp"),
            P(("section", "dp")),
            P(("section", "dp"), None),
            P(("section", "dp"), None),
            P(("section", "dp"), None),
            P(("section", "dp"), None),
            P(("section", "dp")),
            P(("section", "dp"), None),
            P(("section", "dp"), None),
        ),
        out_specs=(
            P(None, "dp", "section", None),
            P(None, "dp", "section", None),
            P(("section", "dp")),
            P(("section", "dp"), None),
            P(("section", "dp"), None),
            P(("section", "dp"), None),
            P(("section", "dp"), None),
            P(("section", "dp")),
            P(("section", "dp"), None),
            P(("section", "dp"), None),
        ),
        check_vma=False,
    )
```

profile of v0, /device:TPU:1, one launch (start us, length us, event | category | flops | bytes accessed | tf_op | source)
XLA Modules:
  0.0 2268.5 jit_solution(333491187392769116)
XLA Ops:
  16.3 72.4 %all-reduce.5 = (bf16[1024]{0:T(1024)(128)(2,1)S(1)}, bf16[1024]{0:T(1024)(128)(2,1)S(1)}) all-reduce(bf16[1024]{0:T(1024)(128)(2,1)S(1)} %dynamic-update-slice, bf16[1024]{0:T(1024)(128)(2,1)S(1)} %dynamic-update-slice.1), channel_id=1, replica_groups=mesh['section'=4,'dp'=32] {'dp'}, use_global_device_ids=true, to_apply=%add | all-reduce | flops 2048 | bytes 8192
  88.6 65.9 %all_gather.33 = bf16[1024,128]{1,0:T(8,128)(2,1)S(1)} all-gather(bf16[32,128]{1,0:T(8,128)(2,1)S(1)} %convert_element_type.797), channel_id=1, replica_groups=mesh['section'=4,'dp'=32] {'dp'}, dimensions={0}, use_global_device_ids=true | all-gather | bytes 270336 | tf_op jit(solution)/shard_map/all_gather | solution.py:220
  154.5 68.0 %all_gather.34 = bf16[1024,128]{1,0:T(8,128)(2,1)S(1)} all-gather(bf16[32,128]{1,0:T(8,128)(2,1)S(1)} %convert_element_type.798), channel_id=1, replica_groups=mesh['section'=4,'dp'=32] {'dp'}, dimensions={0}, use_global_device_ids=true | all-gather | bytes 270336 | tf_op jit(solution)/shard_map/all_gather | solution.py:219
  222.5 86.4 %all-gather.7.cloned.1.call-done = bf16[1024,1024]{1,0:T(8,128)(2,1)} async-done(((bf16[32,1024]{1,0:T(8,128)(2,1)}), bf16[1024,1024]{1,0:T(8,128)(2,1)}) %all-gather.7.cloned.1.call-update) | async-done | bytes 2097168 | tf_op jit(solution)/shard_map/all_gather | solution.py:221
  308.9 212.8 %all-gather.9.cloned.1.call-done = bf16[1024,4096]{1,0:T(8,128)(2,1)} async-done(((bf16[32,4096]{1,0:T(8,128)(2,1)}), bf16[1024,4096]{1,0:T(8,128)(2,1)}) %all-gather.9.cloned.1.call-update) | async-done | bytes 8388624 | tf_op jit(solution)/shard_map/all_gather | solution.py:223
  521.7 190.1 %all-gather.11.cloned.1.call-done = bf16[4096,1024]{1,0:T(8,128)(2,1)} async-done(((bf16[128,1024]{1,0:T(8,128)(2,1)}), bf16[4096,1024]{1,0:T(8,128)(2,1)}) %all-gather.11.cloned.1.call-update) | async-done | bytes 8388624 | tf_op jit(solution)/shard_map/all_gather | solution.py:224
  749.3 36.1 %conditional.11 = (bf16[128,1024]{1,0:T(8,128)(2,1)}, f32[128,1024]{1,0:T(8,128)}, f32[128,1]{0,1:T(1,128)}, bf16[128,1024]{1,0:T(8,128)(2,1)}, f32[8,128,128]{1...) conditional(s32[]{:T(128)} %convert_element_type.804, ...), branch_computations={%region_7.8_spmd, %region_8.14_spmd} | conditional | flops 2824801024 | bytes 72948360 | solution.py:247
  821.3 35.4 %conditional.12 = (bf16[128,1024]{1,0:T(8,128)(2,1)}, f32[128,1024]{1,0:T(8,128)}, f32[128,1]{0,1:T(1,128)}, bf16[128,1024]{1,0:T(8,128)(2,1)}, f32[8,128,128]{1...) conditional(s32[]{:T(128)} %convert_element_type.805, ...), branch_computations={%region_14.15_spmd, %region_15.21_spmd} | conditional | flops 2824801024 | bytes 72948360 | solution.py:247
  895.8 12.8 conditional.13
  974.0 24.2 %conditional.15 = (bf16[128,1024]{1,0:T(8,128)(2,1)}, f32[1024]{0:T(1024)S(1)}, f32[1024,1024]{1,0:T(8,128)}, f32[1024,128]{1,0:T(8,128)}, f32[1024,128]{1,0:T(8...) conditional(s32[]{:T(128)} %convert_element_type.808, ...), branch_computations={%region_35.36_spmd, %region_36.42_spmd} | conditional | flops 5647547392 | bytes 118817880 | solution.py:289
  1013.3 26.1 %conditional.16 = (bf16[128,1024]{1,0:T(8,128)(2,1)}, f32[1024]{0:T(1024)S(1)}, f32[1024,1024]{1,0:T(8,128)}, f32[1024,128]{1,0:T(8,128)}, f32[1024,128]{1,0:T(8...) conditional(s32[]{:T(128)} %convert_element_type.809, ...), branch_computations={%region_42.43_spmd, %region_43.49_spmd} | conditional | flops 5647547392 | bytes 148194496 | solution.py:289
  1041.3 33.1 %collective-permute-done.5 = bf16[128,1024]{1,0:T(8,128)(2,1)} collective-permute-done((bf16[128,1024]{1,0:T(8,128)(2,1)}, bf16[128,1024]{1,0:T(8,128)(2,1)}, u32[]{:S(2)}, u32[]{:S(2)}) %collective-permute-start.5) | collective-permute-done | bytes 262176 | tf_op jit(solution)/shard_map/ppermute | solution.py:19
  1074.4 51.4 %conditional.17 = (bf16[128,1024]{1,0:T(8,128)(2,1)}, f32[1024]{0:T(1024)}, f32[1024,1024]{1,0:T(8,128)}, f32[1024,128]{1,0:T(8,128)}, f32[1024,128]{1,0:T(8,128...) conditional(s32[]{:T(128)} %convert_element_type.810, ...), branch_computations={%region_49.50_spmd, %region_50.56_spmd} | conditional | flops 5647547392 | bytes 148178080 | solution.py:289
  1135.3 50.9 %conditional.18 = (bf16[128,1024]{1,0:T(8,128)(2,1)}, f32[1024]{0:T(1024)S(1)}, f32[1024,1024]{1,0:T(8,128)}, f32[1024,128]{1,0:T(8,128)}, f32[1024,128]{1,0:T(8...) conditional(s32[]{:T(128)} %convert_element_type.811, ...), branch_computations={%region_56.57_spmd, %region_57.63_spmd} | conditional | flops 5647547392 | bytes 148194496 | solution.py:289
  1195.7 33.4 %conditional.19 = (bf16[128,1024]{1,0:T(8,128)(2,1)}, f32[1024]{0:T(1024)}, f32[1024,1024]{1,0:T(8,128)}, f32[1024,128]{1,0:T(8,128)}, f32[1024,128]{1,0:T(8,128...) conditional(s32[]{:T(128)} %convert_element_type.812, ...), branch_computations={%region_63.64_spmd, %region_64.70_spmd} | conditional | flops 5647547392 | bytes 148178080 | solution.py:289
  1255.4 30.6 %add_convert_fusion.1 = bf16[1024,4096]{1,0:T(8,128)(2,1)} fusion(f32[1024,4096]{1,0:T(8,128)} %get-tuple-element.2129, f32[1024,4096]{1,0:T(8,128)} %get-tuple-element.2128, f32[1024,4096]{1,0:T(8,128)} %get-tuple-element.2127, f32[1024,4096]{1,0:T(8,128)} %get-tuple-element.2125, f32[1024,4096]{1,0:T(8,128)} %get-tuple-element.2126), kind=kLoop, calls=%fused_computation.691 | loop fusion | flops 20971520 | bytes 92274688 | tf_op jit(solution)/shard_map/convert_element_type | solution.py:316
  1286.1 30.8 %add_convert_fusion = bf16[4096,1024]{1,0:T(8,128)(2,1)} fusion(f32[4096,1024]{1,0:T(8,128)} %get-tuple-element.2134, f32[4096,1024]{1,0:T(8,128)} %get-tuple-element.2133, f32[4096,1024]{1,0:T(8,128)} %get-tuple-element.2132, f32[4096,1024]{1,0:T(8,128)} %get-tuple-element.2130, f32[4096,1024]{1,0:T(8,128)} %get-tuple-element.2131), kind=kLoop, calls=%fused_computation.690 | loop fusion | flops 20971520 | bytes 92274688 | tf_op jit(solution)/shard_map/convert_element_type | solution.py:319
  1319.5 14.6 all-to-all-start
  1353.8 67.5 %all-reduce.4 = (bf16[1024]{0:T(1024)(128)(2,1)S(1)}, bf16[1024]{0:T(1024)(128)(2,1)S(1)}) all-reduce(bf16[1024]{0:T(1024)(128)(2,1)S(1)} %add_convert_fusion.7, bf16[1024]{0:T(1024)(128)(2,1)S(1)} %add_convert_fusion.6), channel_id=2, replica_groups=mesh['section'=4,'dp'=32] {'dp'}, use_global_device_ids=true, to_apply=%region_70.71.clone | all-reduce | flops 2048 | bytes 8192
  1424.5 106.3 %reduce-scatter.11.cloned.1.call-done = bf16[32,128]{1,0:T(8,128)(2,1)} async-done(((bf16[1024,128]{1,0:T(8,128)(2,1)}), bf16[32,128]{1,0:T(8,128)(2,1)}) %reduce-scatter.11.cloned.1.call-update) | async-done | bytes 8208 | tf_op jit(solution)/shard_map/reduce_scatter | solution.py:306
  1532.1 164.6 %reduce-scatter.7.cloned.1.call-done = bf16[32,1024]{1,0:T(8,128)(2,1)} async-done(((bf16[1024,1024]{1,0:T(8,128)(2,1)}), bf16[32,1024]{1,0:T(8,128)(2,1)}) %reduce-scatter.7.cloned.1.call-update) | async-done | bytes 65552 | tf_op jit(solution)/shard_map/reduce_scatter | solution.py:300
  1698.2 162.4 %reduce-scatter.13.cloned.1.call-done = bf16[32,1024]{1,0:T(8,128)(2,1)} async-done(((bf16[1024,1024]{1,0:T(8,128)(2,1)}), bf16[32,1024]{1,0:T(8,128)(2,1)}) %reduce-scatter.13.cloned.1.call-update) | async-done | bytes 65552 | tf_op jit(solution)/shard_map/reduce_scatter | solution.py:309
  1862.1 200.1 %reduce-scatter.15.cloned.1.call-done = bf16[32,4096]{1,0:T(8,128)(2,1)} async-done(((bf16[1024,4096]{1,0:T(8,128)(2,1)}), bf16[32,4096]{1,0:T(8,128)(2,1)}) %reduce-scatter.15.cloned.1.call-update) | async-done | bytes 262160 | tf_op jit(solution)/shard_map/reduce_scatter | solution.py:315
  2063.9 195.8 %reduce-scatter.17.cloned.1.call-done = bf16[128,1024]{1,0:T(8,128)(2,1)} async-done(((bf16[4096,1024]{1,0:T(8,128)(2,1)}), bf16[128,1024]{1,0:T(8,128)(2,1)}) %reduce-scatter.17.cloned.1.call-update) | async-done | bytes 262160 | tf_op jit(solution)/shard_map/reduce_scatter | solution.py:318
  (794 shorter events, 556.7 us)
Async XLA Ops:
  7.2 704.7 %copy-start.120 = (bf16[2,1,128,1024]{3,2,1,0:T(8,128)(2,1)S(1)}, bf16[2,1,128,1024]{3,2,1,0:T(8,128)(2,1)}, u32[]{:S(2)}) copy-start(bf16[2,1,128,1024]{3,2,1,0:T(8,128)(2,1)} %param.31) | copy-start | bytes 1572868
  7.2 704.7 %copy-start.206 = (s32[2,1]{0,1:T(1,128)S(1)}, s32[2,1]{0,1:T(1,128)}, u32[]{:S(2)}) copy-start(s32[2,1]{0,1:T(1,128)} %param.33) | copy-start | bytes 28
  7.3 215.3 %all-gather.5.cloned.1.call-start = ((), (), s32[]{:S(2)}) async-start(), calls=%async_computation.8 | async-start | bytes 2162688 | tf_op jit(solution)/shard_map/all_gather | solution.py:218
  8.9 300.0 %all-gather.7.cloned.1.call-start = ((), (), s32[]{:S(2)}) async-start(), calls=%async_computation.9 | async-start | bytes 2162688 | tf_op jit(solution)/shard_map/all_gather | solution.py:221
  10.5 511.2 %all-gather.9.cloned.1.call-start = ((), (), s32[]{:S(2)}) async-start(), calls=%async_computation.10 | async-start | bytes 8650752 | tf_op jit(solution)/shard_map/all_gather | solution.py:223
  12.4 699.4 %all-gather.11.cloned.1.call-start = ((), (), s32[]{:S(2)}) async-start(), calls=%async_computation.11 | async-start | bytes 8650752 | tf_op jit(solution)/shard_map/all_gather | solution.py:224
  14.2 1409.0 %reduce-scatter.9.cloned.1.call-start = ((), (), s32[]{:S(2)}) async-start(), calls=%async_computation.13 | async-start | bytes 270336 | tf_op jit(solution)/shard_map/reduce_scatter | solution.py:303
  222.5 489.4 %copy-start.32 = (bf16[1024,128]{1,0:T(8,128)(2,1)}, bf16[1024,128]{1,0:T(8,128)(2,1)S(1)}, u32[]{:S(2)}) copy-start(bf16[1024,128]{1,0:T(8,128)(2,1)S(1)} %all_gather.34) | copy-start | bytes 786436
  722.9 25.5 %collective-permute-start = (bf16[128,1024]{1,0:T(8,128)(2,1)}, bf16[128,1024]{1,0:T(8,128)(2,1)S(1)}, u32[]{:S(2)}, u32[]{:S(2)}) collective-permute-start(bf16[128,1024]{1,0:T(8,128)(2,1)} %get-tuple-element.2010), channel_id=1, source_target_pairs={{0,32},{32,64},{64,96},{1,33},{33,65},{65,97},{2,34},{34,66},{66,9... | collective-permute-start | bytes 786440 | tf_op jit(solution)/shard_map/ppermute | solution.py:19
  785.4 35.2 %collective-permute-start.1 = (bf16[128,1024]{1,0:T(8,128)(2,1)}, bf16[128,1024]{1,0:T(8,128)(2,1)S(1)}, u32[]{:S(2)}, u32[]{:S(2)}) collective-permute-start(bf16[128,1024]{1,0:T(8,128)(2,1)} %get-tuple-element.2011), channel_id=1, source_target_pairs={{0,32},{32,64},{64,96},{1,33},{33,65},{65,97},{2,34},{34,66},{66,9... | collective-permute-start | bytes 786440 | tf_op jit(solution)/shard_map/ppermute | solution.py:19
  856.7 38.5 %collective-permute-start.2 = (bf16[128,1024]{1,0:T(8,128)(2,1)}, bf16[128,1024]{1,0:T(8,128)(2,1)S(1)}, u32[]{:S(2)}, u32[]{:S(2)}) collective-permute-start(bf16[128,1024]{1,0:T(8,128)(2,1)} %get-tuple-element.2012), channel_id=1, source_target_pairs={{0,32},{32,64},{64,96},{1,33},{33,65},{65,97},{2,34},{34,66},{66,9... | collective-permute-start | bytes 786440 | tf_op jit(solution)/shard_map/ppermute | solution.py:19
  908.6 26.5 %collective-permute-start.3 = (bf16[128,1024]{1,0:T(8,128)(2,1)}, bf16[128,1024]{1,0:T(8,128)(2,1)S(1)}, u32[]{:S(2)}, u32[]{:S(2)}) collective-permute-start(bf16[128,1024]{1,0:T(8,128)(2,1)} %get-tuple-element.2013), channel_id=1, source_target_pairs={{0,32},{32,64},{64,96},{1,33},{33,65},{65,97},{2,34},{34,66},{66,9... | collective-permute-start | bytes 786440 | tf_op jit(solution)/shard_map/ppermute | solution.py:19
  998.3 15.0 collective-permute-start.4
  1039.4 35.0 %copy-start.199 = (f32[1024]{0:T(1024)}, f32[1024]{0:T(1024)S(1)}, u32[]{:S(2)}) copy-start(f32[1024]{0:T(1024)S(1)} %get-tuple-element.2096) | copy-start | bytes 12292
  1039.4 35.0 %collective-permute-start.5 = (bf16[128,1024]{1,0:T(8,128)(2,1)}, bf16[128,1024]{1,0:T(8,128)(2,1)}, u32[]{:S(2)}, u32[]{:S(2)}) collective-permute-start(bf16[128,1024]{1,0:T(8,128)(2,1)} %get-tuple-element.2091), channel_id=1, source_target_pairs={{32,0},{64,32},{96,64},{33,1},{65,33},{97,65},{34,2},{66,34},{98,6... | collective-permute-start | bytes 786440 | tf_op jit(solution)/shard_map/ppermute | solution.py:19
  1125.8 9.5 collective-permute-start.6
  1186.2 9.5 collective-permute-start.7
  1231.6 299.3 %reduce-scatter.11.cloned.1.call-start = ((), (), s32[]{:S(2)}) async-start(), calls=%async_computation.14 | async-start | bytes 270336 | tf_op jit(solution)/shard_map/reduce_scatter | solution.py:306
  1234.1 462.6 %reduce-scatter.7.cloned.1.call-start = ((), (), s32[]{:S(2)}) async-start(), calls=%async_computation.12 | async-start | bytes 2162688 | tf_op jit(solution)/shard_map/reduce_scatter | solution.py:300
  1244.7 615.9 %reduce-scatter.13.cloned.1.call-start = ((), (), s32[]{:S(2)}) async-start(), calls=%async_computation.15 | async-start | bytes 2162688 | tf_op jit(solution)/shard_map/reduce_scatter | solution.py:309
  1255.3 806.8 %reduce-scatter.15.cloned.1.call-start = ((), (), s32[]{:S(2)}) async-start(), calls=%async_computation.16 | async-start | bytes 8650752 | tf_op jit(solution)/shard_map/reduce_scatter | solution.py:315
  1286.0 973.7 %reduce-scatter.17.cloned.1.call-start = ((), (), s32[]{:S(2)}) async-start(), calls=%async_computation.17 | async-start | bytes 8650752 | tf_op jit(solution)/shard_map/reduce_scatter | solution.py:318
  1319.5 24.1 %all-to-all-start = ((bf16[2,128,1024]{2,0,1:T(2,128)(2,1)}), bf16[2,128,1024]{2,0,1:T(2,128)(2,1)S(1)}, u32[]{:S(2)}, u32[]{:S(2)}) async-start(bf16[2,128,1024]{2,0,1:T(2,128)(2,1)} %copy.324), calls=%async_computation | async-start | bytes 1048576 | tf_op jit(solution)/shard_map/all_to_all | solution.py:323
  1346.1 76.4 %all-to-all-start.1 = ((bf16[2,128,1024]{2,0,1:T(2,128)(2,1)}), bf16[2,128,1024]{2,0,1:T(2,128)(2,1)S(1)}, u32[]{:S(2)}, u32[]{:S(2)}) async-start(bf16[2,128,1024]{2,0,1:T(2,128)(2,1)} %copy.356), calls=%async_computation.1 | async-start | bytes 1048576 | tf_op jit(solution)/shard_map/all_to_all | solution.py:324
  (180 other events, 878.0 us)
Sparse Core Ops, SparseCore 0:
  10.3 141.1 all-gather.4
  153.7 155.1 all-gather.6
  311.2 210.5 all-gather.8
  523.8 187.9 all-gather.10
  1231.7 141.3 reduce-scatter.8
  1375.4 155.3 reduce-scatter.10
  1533.2 163.4 reduce-scatter.6
  1699.2 161.3 reduce-scatter.12
  1863.0 199.1 reduce-scatter.14
  2064.4 195.2 reduce-scatter.16
where the time goes:
time: 2300 us; the launch traced here: 2270 us
  waiting for transfers between devices  1390 us (60%)
  blocking collectives  274 us (12%)
  other arithmetic  208 us (9%)
  local copies, waits for them, and re-layouts  199 us (9%)
  matrix products  125 us (5%)
  starting transfers between devices  40.3 us (2%)
    all_gather x1, waiting for transfers between devices, body(): lax.all_gather(w_up.astype(jnp.bfloat16), 'dp', axis=0, tiled=True)  213 us
    reduce_scatter x1, waiting for transfers between devices, body(): lax.psum_scatter(totals[6].astype(jnp.bfloat16), 'dp', scatter_dimension=...  200 us
    reduce_scatter x1, waiting for transfers between devices, body(): lax.psum_scatter(totals[7].astype(jnp.bfloat16), 'dp', scatter_dimension=...  196 us
    all_gather x1, waiting for transfers between devices, body(): lax.all_gather(w_down.astype(jnp.bfloat16), 'dp', axis=0, tiled=True)  190 us
    reduce_scatter x1, waiting for transfers between devices, body(): lax.psum_scatter(totals[1].astype(jnp.bfloat16), 'dp', scatter_dimension=...  165 us
    reduce_scatter x1, waiting for transfers between devices, body(): lax.psum_scatter(totals[4].astype(jnp.bfloat16), 'dp', scatter_dimension=...  162 us
    unnamed x2, blocking collectives  140 us
    another operation x90, local copies, waits for them, and re-layouts  111 us
  transfers between devices with their start and end apart: 20, of which 13 were waited for; matrix products, arithmetic and copies ran while one was open for 10% of the time, Pallas kernels for 0%

commit v1 on v0

v1 whole, which is shorter than its diff:
```python
import functools

import jax
import jax.numpy as jnp
from jax import lax
from jax.experimental import pallas as pl
from jax.experimental.pallas import tpu as pltpu
from jax.sharding import PartitionSpec as P

D = 1024
HEADS = 8
HD = 128
FF = 4096
LAYERS = 4
SEQ = 128
MICRO = 2
NORM_EPS = 1e-06
NEG_FILL = -1000000000.0
W1 = D + 2 * HD + HD + D
BF = jnp.bfloat16
F32 = jnp.float32
MESH = pl.DeviceIdType.MESH


class Role:
    def __init__(self):
        section = lax.axis_index("section")
        dp = lax.axis_index("dp")
        self.c = section % 2
        self.x_lo = dp % 2
        self.x = (section // 2) * 2 + self.x_lo
        self.z = (dp // 2) % 4
        self.y = dp // 8
        self.native = self.c == self.x_lo

    def dev(self, x, y, z, c):
        return ((x // 2) * 2 + c, (y * 4 + z) * 2 + x % 2)

    def along(self, axis, step):
        if axis == 0:
            return self.dev(self.x, (self.y + step + 4) % 4, self.z, self.c)
        return self.dev(self.x, self.y, (self.z + step + 4) % 4, self.c)

    def partner(self):
        return self.dev(self.x, self.y, self.z, 1 - self.c)

    def swap(self):
        return self.dev(self.x + 1 - 2 * self.x_lo, self.y, self.z, 1 - self.c)


def remote(src, dst, sems, device):
    return pltpu.make_async_remote_copy(
        src_ref=src, dst_ref=dst, send_sem=sems[0], recv_sem=sems[1], device_id=device, device_id_type=MESH
    )


def greet(devices):
    barrier = pltpu.get_barrier_semaphore()
    for device in devices:
        pl.semaphore_signal(barrier, inc=1, device_id=device, device_id_type=MESH)
    pl.semaphore_wait(barrier, len(devices))


N_GATHER = 12


def gather_chunks(shards, fulls):
    chunks = []
    for which, cuts in ((0, 1), (1, 2), (2, 2)):
        wide = shards[which].shape[-1] // cuts
        for cut in range(cuts):
            chunks.append((shards[which], fulls[which], cut * wide, wide))
    return chunks


def gather_kernel(s1, s2, s3, act, f1, f2, f3, act_out, send, recv, swap_send, swap_recv, local):
    role = Role()
    y, z, c = role.y, role.z, role.c
    place = (y, z)
    greet([role.along(0, 1), role.along(0, -1), role.along(1, 1), role.along(1, -1), role.partner(), role.swap()])
    chunks = gather_chunks((s1, s2, s3), (f1, f2, f3))
    count = len(chunks)

    def moved(step):
        shard, full, start, wide = chunks[step]
        return shard.at[:, :, pl.ds(start, wide)], full

    def own_copies(step, owner):
        src, full = moved(step)
        start, wide = chunks[step][2:]
        return (
            remote(src, full.at[y, z, owner, :, :, pl.ds(start, wide)], (swap_send.at[step], swap_recv.at[step]), role.swap()),
            pltpu.make_async_copy(src, full.at[y, z, owner, :, :, pl.ds(start, wide)], local.at[step]),
        )

    act_far = remote(act, act_out, (swap_send.at[count], swap_recv.at[count]), role.swap())
    act_near = pltpu.make_async_copy(act, act_out, local.at[count])

    @pl.when(role.native)
    def _():
        for step in range(count):
            own_copies(step, c)[1].start()
        act_near.start()

    @pl.when(jnp.logical_not(role.native))
    def _():
        for step in range(count):
            own_copies(step, 1 - c)[0].start()
        act_far.start()

    def piece(step, half, first, second, cols=None):
        full, start, wide = chunks[step][1:]
        if cols is not None:
            near = (wide // HD + 1) // 2 * HD
            start, wide = (start, near) if cols[0] == 0 else (start + near, wide - near)
        index = (first, second) if half == 0 else (second, first)
        return full.at[index[0], index[1], c, half, :, pl.ds(start, wide)]

    def hop(step, half, number, view, device):
        at = (step * 2 + half) * N_GATHER + number
        return remote(view, view, (send.at[at], recv.at[at]), device)

    def copies(step, half):
        one, two = half, 1 - half
        p, s = place[one], place[two]
        nxt, prv, opp = (p + 1) % 4, (p + 3) % 4, (p + 2) % 4
        snx, spv, sop = (s + 1) % 4, (s + 3) % 4, (s + 2) % 4
        up1, down1 = role.along(one, 1), role.along(one, -1)
        up2, down2 = role.along(two, 1), role.along(two, -1)
        every = slice(None)
        low, high = pl.ds(0, 2), pl.ds(2, 2)
        sends = [
            hop(step, half, 0, piece(step, half, p, s), up1),
            hop(step, half, 1, piece(step, half, p, s), down1),
            hop(step, half, 2, piece(step, half, prv, s, (0,)), up1),
            hop(step, half, 3, piece(step, half, nxt, s, (1,)), down1),
            hop(step, half, 4, piece(step, half, every, s), up2),
            hop(step, half, 5, piece(step, half, every, s), down2),
            hop(step, half, 6, piece(step, half, low, spv), up2),
            hop(step, half, 7, piece(step, half, high, snx), down2),
            hop(step, half, 8, piece(step, half, every, s), role.partner()),
            hop(step, half, 9, piece(step, half, every, spv), role.partner()),
            hop(step, half, 10, piece(step, half, every, snx), role.partner()),
            hop(step, half, 11, piece(step, half, every, sop), role.partner()),
        ]
        return sends

    def start(step, half, numbers):
        made = copies(step, half)
        for number in numbers:
            made[number].start()

    def landed(step, half, numbers):
        made = copies(step, half)
        for number in numbers:
            made[number].wait_recv()

    def stage(step, level):
        if level == 0:
            @pl.when(role.native)
            def _():
                own_copies(step, c)[1].wait()

            @pl.when(jnp.logical_not(role.native))
            def _():
                own_copies(step, 1 - c)[0].wait()

            for half in (0, 1):
                start(step, half, (0, 1))
        elif level == 1:
            for half in (0, 1):
                landed(step, half, (0, 1))
                start(step, half, (2, 3))
        elif level == 2:
            for half in (0, 1):
                landed(step, half, (2, 3))
                start(step, half, (4, 5, 8))
        elif level == 3:
            for half in (0, 1):
                landed(step, half, (4, 5))
                start(step, half, (6, 7, 9, 10))
        elif level == 4:
            for half in (0, 1):
                landed(step, half, (6, 7))
                start(step, half, (11,))

    for tick in range(count + 4):
        for level in range(5):
            step = tick - level
            if 0 <= step < count:
                stage(step, level)
    for step in range(count):
        for half in (0, 1):
            made = copies(step, half)
            for number in (8, 9, 10, 11):
                made[number].wait_recv()
            for number in range(N_GATHER):
                made[number].wait_send()

    @pl.when(role.native)
    def _():
        act_near.wait()

    @pl.when(jnp.logical_not(role.native))
    def _():
        act_far.wait()


def gather(s1, s2, s3, act):
    steps = 5
    hops = steps * 2 * N_GATHER
    hbm = pl.BlockSpec(memory_space=pl.ANY)
    return pl.pallas_call(
        gather_kernel,
        out_shape=[
            jax.ShapeDtypeStruct((4, 4, 2) + s1.shape, BF),
            jax.ShapeDtypeStruct((4, 4, 2) + s2.shape, BF),
            jax.ShapeDtypeStruct((4, 4, 2) + s3.shape, BF),
            jax.ShapeDtypeStruct(act.shape, BF),
        ],
        in_specs=[hbm] * 4,
        out_specs=[hbm] * 4,
        scratch_shapes=[
            pltpu.SemaphoreType.DMA((hops,)),
            pltpu.SemaphoreType.DMA((hops,)),
            pltpu.SemaphoreType.DMA((steps + 1,)),
            pltpu.SemaphoreType.DMA((steps + 1,)),
            pltpu.SemaphoreType.DMA((steps + 1,)),
        ],
        compiler_params=pltpu.CompilerParams(collective_id=0, has_side_effects=True),
        name="gather_weights",
    )(s1, s2, s3, act)


N_SCATTER = 9


def scatter_kernel(
    g1, g2, g3, fin, ing,
    o1, o2, o3, fin_out, ing_out,
    l1, l2, l3, r1, r2, r3, a1, a2, a3, b1, b2, b3, c1, c2, c3, d1, d2, d3, w1, w2, w3,
    send, recv, swap_send, swap_recv, local, row_send, row_recv, row_local,
):
    role = Role()
    x, y, z, c = role.x, role.y, role.z, role.c
    place = (y, z)
    row = []
    for away in range(4):
        for other in range(2):
            if (away, other) != (0, 0):
                row.append(role.dev((x + away) % 4, y, z, (c + other) % 2))
    greet([role.along(0, 1), role.along(0, -1), role.along(1, 1), role.along(1, -1)] + row)

    rows = SEQ // LAYERS
    home = (fin, ing)
    away_out = (fin_out, ing_out)
    source_x = (3, 0)

    def row_copies(which):
        made = []
        for section in range(LAYERS):
            target_x, target_c = 2 * (section // 2) + c, section % 2
            src = home[which].at[:, pl.ds(section * rows, rows)]
            at = which * LAYERS + section
            self_here = jnp.logical_and(target_x == source_x[which], target_c == c)
            far = remote(src, away_out[which], (row_send.at[at], row_recv.at[which]), role.dev(target_x, y, z, target_c))
            near = pltpu.make_async_copy(src, away_out[which], row_local.at[which])
            made.append((self_here, far, near))
        return made

    def row_start(which):
        @pl.when(x == source_x[which])
        def _():
            for self_here, far, near in row_copies(which):
                @pl.when(self_here)
                def _():
                    near.start()

                @pl.when(jnp.logical_not(self_here))
                def _():
                    far.start()

    def row_finish(which):
        kept = jnp.logical_and(x == source_x[which], role.x_lo == c)
        kept = jnp.logical_and(kept, (x // 2) * 2 + c == x)

        @pl.when(x == source_x[which])
        def _():
            for self_here, far, near in row_copies(which):
                @pl.when(self_here)
                def _():
                    near.wait()

                @pl.when(jnp.logical_not(self_here))
                def _():
                    far.wait_send()

        @pl.when(jnp.logical_not(kept))
        def _():
            row_copies(which)[0][1].wait_recv()

    row_start(0)
    row_start(1)

    grads, outs = (g1, g2, g3), (o1, o2, o3)
    mine, theirs = (l1, l2, l3), (r1, r2, r3)
    bufs_a, bufs_b, bufs_c, bufs_d, bufs_w = (a1, a2, a3), (b1, b2, b3), (c1, c2, c3), (d1, d2, d3), (w1, w2, w3)
    chunks = []
    for which, cuts in ((2, 2), (1, 2), (0, 1)):
        wide = grads[which].shape[-1] // cuts
        for cut in range(cuts):
            chunks.append((which, cut * wide, wide))
    count = len(chunks)

    def core_copies(step):
        which, start, wide = chunks[step]
        cols = pl.ds(start, wide)
        at = step * 2 * N_SCATTER
        return (
            remote(grads[which].at[:, :, 1 - c, :, :, cols], theirs[which].at[:, :, :, :, cols], (send.at[at], recv.at[at]), role.partner()),
            pltpu.make_async_copy(grads[which].at[:, :, c, :, :, cols], mine[which].at[:, :, :, :, cols], local.at[step]),
        )

    for step in range(count):
        for copy in core_copies(step):
            copy.start()

    def near_far(step, part):
        start, wide = chunks[step][1:]
        near = (wide // HD + 1) // 2 * HD
        return pl.ds(start, near) if part == 0 else pl.ds(start + near, wide - near)

    def piece(step, half, first, second, part=None):
        which, start, wide = chunks[step]
        index = (first, second) if half == 0 else (second, first)
        cols = pl.ds(start, wide) if part is None else near_far(step, part)
        return mine[which].at[index[0], index[1], half, :, cols]

    def copies(step, half):
        which, start, wide = chunks[step]
        cols = pl.ds(start, wide)
        one, two = half, 1 - half
        p, s = place[one], place[two]
        nxt, prv, opp = (p + 1) % 4, (p + 3) % 4, (p + 2) % 4
        snx, spv, sop = (s + 1) % 4, (s + 3) % 4, (s + 2) % 4
        up1, down1 = role.along(one, 1), role.along(one, -1)
        up2, down2 = role.along(two, 1), role.along(two, -1)
        every, low, high = slice(None), pl.ds(0, 2), pl.ds(2, 2)
        a, b, cc, d = bufs_a[which], bufs_b[which], bufs_c[which], bufs_d[which]

        def hop(number, src, dst, device):
            at = (step * 2 + half) * N_SCATTER + 1 + number
            return remote(src, dst, (send.at[at], recv.at[at]), device)

        return [
            hop(0, piece(step, half, opp, low), a.at[half, 0, :, :, cols], up1),
            hop(1, piece(step, half, opp, high), a.at[half, 1, :, :, cols], down1),
            hop(2, piece(step, half, nxt, every), b.at[half, 0, :, :, cols], up1),
            hop(3, piece(step, half, prv, every), b.at[half, 1, :, :, cols], down1),
            hop(4, piece(step, half, p, sop, 0), cc.at[half, 0, :, near_far(step, 0)], up2),
            hop(5, piece(step, half, p, sop, 1), cc.at[half, 1, :, near_far(step, 1)], down2),
            hop(6, piece(step, half, p, snx), d.at[half, 0, :, cols], up2),
            hop(7, piece(step, half, p, spv), d.at[half, 1, :, cols], down2),
        ]

    def stage(step, level):
        which, start, wide = chunks[step]
        cols = pl.ds(start, wide)
        a, b, cc, d = bufs_a[which], bufs_b[which], bufs_c[which], bufs_d[which]
        if level == 0:
            far, near = core_copies(step)
            far.wait_recv()
            near.wait()
            mine_view, theirs_view = mine[which], theirs[which]

            @pl.loop(0, 16)
            def _(at):
                index = (at // 4, at % 4, slice(None), slice(None), cols)
                mine_view[index] = mine_view[index] + theirs_view[index]

        for half in (0, 1):
            made = copies(step, half)
            one, two = half, 1 - half
            p, s = place[one], place[two]
            nxt, prv = (p + 1) % 4, (p + 3) % 4
            snx, spv = (s + 1) % 4, (s + 3) % 4
            if level == 0:
                made[0].start()
                made[1].start()
            elif level == 1:
                made[0].wait_recv()
                made[1].wait_recv()
                for i in range(2):
                    up = piece(step, half, nxt, i)
                    up[...] = up[...] + a[half, 0, i, :, cols]
                    down = piece(step, half, prv, 2 + i)
                    down[...] = down[...] + a[half, 1, i, :, cols]
                made[2].start()
                made[3].start()
            elif level == 2:
                made[2].wait_recv()
                made[3].wait_recv()
                for i in range(4):
                    here = piece(step, half, p, i)
                    total = here[...].astype(F32) + b[half, 0, i, :, cols].astype(F32) + b[half, 1, i, :, cols].astype(F32)
                    here[...] = total.astype(BF)
                made[4].start()
                made[5].start()
            elif level == 3:
                made[4].wait_recv()
                made[5].wait_recv()
                up = piece(step, half, p, snx, 0)
                up[...] = up[...] + cc[half, 0, :, near_far(step, 0)]
                down = piece(step, half, p, spv, 1)
                down[...] = down[...] + cc[half, 1, :, near_far(step, 1)]
                made[6].start()
                made[7].start()
            elif level == 4:
                made[6].wait_recv()
                made[7].wait_recv()
                total = (
                    piece(step, half, p, s)[...].astype(F32)
                    + d[half, 0, :, cols].astype(F32)
                    + d[half, 1, :, cols].astype(F32)
                )

                @pl.when(role.native)
                def _():
                    outs[which][half, :, cols] = total

                @pl.when(jnp.logical_not(role.native))
                def _():
                    piece(step, half, p, s)[...] = total.astype(BF)
                    swapped(step, half).start()

    def swapped(step, half):
        which, start, wide = chunks[step]
        return remote(
            piece(step, half, y if half == 0 else z, z if half == 0 else y),
            bufs_w[which].at[half, :, pl.ds(start, wide)],
            (swap_send.at[step * 2 + half], swap_recv.at[step * 2 + half]),
            role.swap(),
        )

    for tick in range(count + 4):
        for level in range(4, -1, -1):
            step = tick - level
            if 0 <= step < count:
                stage(step, level)

    @pl.when(jnp.logical_not(role.native))
    def _():
        for step in range(count):
            which, start, wide = chunks[step]
            for half in (0, 1):
                swapped(step, half).wait()
                outs[which][half, :, pl.ds(start, wide)] = bufs_w[which][half, :, pl.ds(start, wide)].astype(F32)

    for step in range(count):
        core_copies(step)[0].wait_send()
        for half in (0, 1):
            for copy in copies(step, half):
                copy.wait_send()
    row_finish(0)
    row_finish(1)


def scatter(g1, g2, g3, fin, ing):
    steps = 5
    hops = steps * 2 * N_SCATTER
    hbm = pl.BlockSpec(memory_space=pl.ANY)
    vmem = pl.BlockSpec(memory_space=pltpu.VMEM)
    tails = [g.shape[4:] for g in (g1, g2, g3)]
    heads = ((4, 4, 2), (4, 4, 2), (2, 2, 2), (2, 2, 4), (2, 2), (2, 2), (2,))
    scratch = [pltpu.VMEM(head + tail, BF) for head in heads for tail in tails]
    rows = SEQ // LAYERS
    return pl.pallas_call(
        scatter_kernel,
        out_shape=[jax.ShapeDtypeStruct((2,) + tail, F32) for tail in tails]
        + [jax.ShapeDtypeStruct((MICRO, rows, D), BF)] * 2,
        in_specs=[hbm] * 5,
        out_specs=[vmem] * 3 + [hbm] * 2,
        scratch_shapes=scratch
        + [
            pltpu.SemaphoreType.DMA((hops,)),
            pltpu.SemaphoreType.DMA((hops,)),
            pltpu.SemaphoreType.DMA((steps * 2,)),
            pltpu.SemaphoreType.DMA((steps * 2,)),
            pltpu.SemaphoreType.DMA((steps,)),
            pltpu.SemaphoreType.DMA((2 * LAYERS,)),
            pltpu.SemaphoreType.DMA((2,)),
            pltpu.SemaphoreType.DMA((2,)),
        ],
        compiler_params=pltpu.CompilerParams(collective_id=1, has_side_effects=True, vmem_limit_bytes=60 << 20),
        name="scatter_gradients",
    )(g1, g2, g3, fin, ing)


def plain_dot(left, right):
    return jnp.dot(left, right, preferred_element_type=F32)


def contract_rows(left, right):
    return lax.dot_general(left, right, (((0,), (0,)), ((), ())), preferred_element_type=F32)


def times_transpose(left, right):
    return lax.dot_general(left, right, (((1,), (1,)), ((), ())), preferred_element_type=F32)


def rms_parts(values):
    factor = lax.rsqrt(jnp.mean(values * values, axis=-1, keepdims=True) + NORM_EPS)
    return values * factor, factor


def norm_back(grad_normed, normed, factor):
    return factor * (grad_normed - normed * jnp.mean(grad_normed * normed, axis=-1, keepdims=True))


def split_weights(fulls):
    first, second, third = fulls
    first = first.reshape(D, W1)
    gains = first[:, D + 2 * HD : D + 2 * HD + 2].astype(F32)
    return (
        gains[:, 0],
        first[:, :D],
        first[:, D : D + HD],
        first[:, D + HD : D + 2 * HD],
        first[:, W1 - D :],
        gains[:, 1],
        second.reshape(D, FF),
        third.reshape(FF, D),
    )


def attention_scores(queries, keys_all, lengths):
    positions = jnp.arange(SEQ)
    allowed = (positions[None, None, :] <= positions[None, :, None]) & (positions[None, None, :] < lengths[:, None, None])
    scores = jnp.einsum("bthd,bsd->bhts", queries, keys_all, preferred_element_type=F32) * HD ** (-0.5)
    scores = jnp.where(allowed[:, None], scores, NEG_FILL)
    shifted = jnp.exp(scores - jnp.max(scores, axis=-1, keepdims=True))
    return shifted / jnp.sum(shifted, axis=-1, keepdims=True)


def layer_forward(hidden_in, lengths, params):
    attn_gain, w_query, w_key, w_value, w_out, ffn_gain, w_up, w_down = params
    tokens = MICRO * SEQ
    hidden = hidden_in.astype(F32)
    pad_mask = (jnp.arange(SEQ)[None, :] < lengths[:, None]).astype(F32).reshape(tokens, 1)
    normed_a, _ = rms_parts(hidden)
    attn_in = (normed_a * attn_gain).astype(BF)
    queries = plain_dot(attn_in, w_query).astype(BF)
    keys_all = plain_dot(attn_in, w_key).astype(BF)
    values_all = plain_dot(attn_in, w_value).astype(BF)
    probs = attention_scores(
        queries.reshape(MICRO, SEQ, HEADS, HD), keys_all.reshape(MICRO, SEQ, HD), lengths
    )
    mixed = jnp.einsum("bhts,bsd->bthd", probs.astype(BF), values_all.reshape(MICRO, SEQ, HD), preferred_element_type=F32)
    mixed = mixed.reshape(tokens, D).astype(BF)
    after = hidden + pad_mask * plain_dot(mixed, w_out)
    normed_f, _ = rms_parts(after)
    ffn_in = (normed_f * ffn_gain).astype(BF)
    pre_act = plain_dot(ffn_in, w_up)
    act_out = jax.nn.silu(pre_act).astype(BF)
    result = (after + pad_mask * plain_dot(act_out, w_down)).astype(BF)
    return result, (hidden_in, attn_in, queries, keys_all, values_all, probs, mixed, after, ffn_in, pre_act, act_out)


def layer_backward(kept, grad_in, lengths, params):
    attn_gain, w_query, w_key, w_value, w_out, ffn_gain, w_up, w_down = params
    hidden_in, attn_in, queries, keys_all, values_all, probs, mixed, after, ffn_in, pre_act, act_out = kept
    tokens = MICRO * SEQ
    scale = HD ** (-0.5)
    pad_mask = (jnp.arange(SEQ)[None, :] < lengths[:, None]).astype(F32).reshape(tokens, 1)
    normed_a, factor_a = rms_parts(hidden_in.astype(F32))
    normed_f, factor_f = rms_parts(after)
    grad_out = grad_in.astype(F32)
    grad_ffn = (grad_out * pad_mask).astype(BF)
    g_down = contract_rows(act_out, grad_ffn)
    grad_act = times_transpose(grad_ffn, w_down)
    sigmoid = jax.nn.sigmoid(pre_act)
    grad_pre = (grad_act * sigmoid * (1.0 + pre_act * (1.0 - sigmoid))).astype(BF)
    g_up = contract_rows(ffn_in, grad_pre)
    grad_ffn_in = times_transpose(grad_pre, w_up)
    g_ffn_gain = jnp.sum(grad_ffn_in * normed_f, axis=0)
    grad_after = grad_out + norm_back(grad_ffn_in * ffn_gain, normed_f, factor_f)
    grad_attn = (grad_after * pad_mask).astype(BF)
    g_out = contract_rows(mixed, grad_attn)
    grad_mixed = times_transpose(grad_attn, w_out).astype(BF).reshape(MICRO, SEQ, HEADS, HD)
    keys_b, values_b = keys_all.reshape(MICRO, SEQ, HD), values_all.reshape(MICRO, SEQ, HD)
    queries_b = queries.reshape(MICRO, SEQ, HEADS, HD)
    grad_probs = jnp.einsum("bthd,bsd->bhts", grad_mixed, values_b, preferred_element_type=F32)
    grad_values = jnp.einsum("bhts,bthd->bsd", probs.astype(BF), grad_mixed, preferred_element_type=F32).astype(BF)
    grad_scores = (probs * (grad_probs - jnp.sum(probs * grad_probs, axis=-1, keepdims=True))).astype(BF)
    grad_queries = (jnp.einsum("bhts,bsd->bthd", grad_scores, keys_b, preferred_element_type=F32) * scale).astype(BF)
    grad_keys = (jnp.einsum("bhts,bthd->bsd", grad_scores, queries_b, preferred_element_type=F32) * scale).astype(BF)
    grad_queries = grad_queries.reshape(tokens, D)
    grad_keys, grad_values = grad_keys.reshape(tokens, HD), grad_values.reshape(tokens, HD)
    g_query = contract_rows(attn_in, grad_queries)
    g_key = contract_rows(attn_in, grad_keys)
    g_value = contract_rows(attn_in, grad_values)
    grad_attn_in = (
        times_transpose(grad_queries, w_query)
        + times_transpose(grad_keys, w_key)
        + times_transpose(grad_values, w_value)
    )
    g_attn_gain = jnp.sum(grad_attn_in * normed_a, axis=0)
    grad_hidden = grad_after + norm_back(grad_attn_in * attn_gain, normed_a, factor_a)
    gains = jnp.pad(jnp.stack([g_attn_gain, g_ffn_gain], axis=1), ((0, 0), (0, HD - 2)))
    first = jnp.concatenate([g_query, g_key, g_value, gains, g_out], axis=1).astype(BF)
    shaped = (
        first.reshape(4, 4, 2, 2, 16, W1),
        g_up.astype(BF).reshape(4, 4, 2, 2, 16, FF),
        g_down.astype(BF).reshape(4, 4, 2, 2, 64, D),
    )
    return grad_hidden.astype(BF), shaped


def relay(value, distance):
    route = []
    for x in range(4):
        for yz in range(16):
            for c in range(2):
                if 0 <= x + distance < 4:
                    there = x + distance
                    route.append((((x // 2) * 2 + c) * 32 + yz * 2 + x % 2, ((there // 2) * 2 + c) * 32 + yz * 2 + there % 2))
    return lax.ppermute(value, ("section", "dp"), route)


def body(
    inputs, cotangent, lengths, attn_gain, w_query, w_key, w_value, w_out, ffn_gain, w_up, w_down
):
    role = Role()
    tokens = MICRO * SEQ
    gains = jnp.pad(jnp.stack([attn_gain, ffn_gain], axis=1), ((0, 0), (0, HD - 2)))
    first = jnp.concatenate([w_query, w_key, w_value, gains, w_out], axis=1).astype(BF).reshape(2, 16, W1)
    second = w_up.astype(BF).reshape(2, 16, FF)
    third = w_down.astype(BF).reshape(2, 64, D)
    rows = jnp.where(role.x < 2, inputs[:, 0], cotangent[:, 0])
    lengths_rows = jnp.broadcast_to(lengths.astype(BF)[:, :, None], (MICRO, 16, D))
    act = jnp.concatenate([rows, lengths_rows], axis=1)
    f1, f2, f3, act = gather(first, second, third, act)
    start_rows = act[:, :SEQ].reshape(tokens, D)
    lengths_here = act[:, SEQ, 0].astype(jnp.int32)
    params = split_weights((f1, f2, f3))

    hidden = start_rows
    kept = None
    for tick in range(LAYERS):
        def run(operands):
            return layer_forward(operands, lengths_here, params)

        shapes = jax.eval_shape(run, hidden)
        if kept is None:
            kept = jax.tree.map(lambda a: jnp.zeros(a.shape, a.dtype), shapes[1])
        hidden_out, kept = lax.cond(
            role.x == tick, lambda ops: layer_forward(ops[0], lengths_here, params), lambda ops: ops, (hidden, kept)
        )
        hidden = relay(hidden_out, 1) if tick < LAYERS - 1 else hidden_out
    final_full = hidden

    grad = start_rows
    shaped = None
    for tick in range(LAYERS - 1, -1, -1):
        if shaped is None:
            shaped = (
                jnp.zeros((4, 4, 2, 2, 16, W1), BF),
                jnp.zeros((4, 4, 2, 2, 16, FF), BF),
                jnp.zeros((4, 4, 2, 2, 64, D), BF),
            )
        grad, shaped = lax.cond(
            role.x == tick,
            lambda ops: layer_backward(kept, ops[0], lengths_here, params),
            lambda ops: ops,
            (grad, shaped),
        )
        if tick > 0:
            grad = relay(grad, -1)
    o1, o2, o3, final_rows, input_rows = scatter(
        *shaped, final_full.reshape(MICRO, SEQ, D), grad.reshape(MICRO, SEQ, D)
    )
    o1 = o1.reshape(32, W1)
    return (
        final_rows[:, None],
        input_rows[:, None],
        o1[:, D + 2 * HD],
        o1[:, :D],
        o1[:, D : D + HD],
        o1[:, D + HD : D + 2 * HD],
        o1[:, W1 - D :],
        o1[:, D + 2 * HD + 1],
        o2.reshape(32, FF),
        o3.reshape(128, D),
    )


def solution(mesh):
    both = P(("section", "dp"))
    both_rows = P(("section", "dp"), None)
    acts = P(None, "dp", None, None)
    outs = P(None, "dp", "section", None)
    weights = (both, both_rows, both_rows, both_rows, both_rows, both, both_rows, both_rows)
    return jax.shard_map(
        body,
        mesh=mesh,
        in_specs=(acts, acts, P(None, "dp")) + weights,
        out_specs=(outs, outs) + weights,
        check_vma=False,
    )
```

time: 2300 us -> 677 us (0.29)
  waiting for transfers between devices: 1390 us -> 307 us
  blocking collectives: 274 us -> 0 us
  other arithmetic: 208 us -> 23.1 us
  Pallas kernels: 0 us -> 159 us
  local copies, waits for them, and re-layouts: 199 us -> 61.5 us
  matrix products: 125 us -> 58.6 us
    reduce_scatter x6 -> x0, waiting for transfers between devices: 829 us -> none  [the longest x1 200 us: body(): lax.psum_scatter(totals[6].astype(jnp.bfloat16), 'dp', scatter_dimension=...]
    all_gather x4 -> x0, waiting for transfers between devices: 489 us -> none  [the longest x1 213 us: body(): lax.all_gather(w_up.astype(jnp.bfloat16), 'dp', axis=0, tiled=True)]
    ppermute x8 -> x6, waiting for transfers between devices: 60.7 us -> 307 us  [relay(): return lax.ppermute(value, ('section', 'dp'), route)]
    pallas_call x0 -> x2, Pallas kernels: none -> 159 us  [the longest x1 82.1 us: scatter(): pl.pallas_call(scatter_kernel, out_shape=[jax.ShapeDtypeStruct((2,) + tai...]
    unnamed x2 -> x0, blocking collectives: 140 us -> none
    all_gather x2 -> x0, blocking collectives: 134 us -> none  [the longest x1 68 us: body(): lax.all_gather(w_key.astype(jnp.bfloat16), 'dp', axis=0, tiled=True)]
    another operation x90 -> x2, local copies, waits for them, and re-layouts: 111 us -> 0.01 us  [layer_backward(): jnp.stack([g_attn_gain, g_ffn_gain], axis=1)]
    convert_element_type x44 -> x9, other arithmetic: 121 us -> 9.95 us  [the longest x1 1.78 us: body(): third = w_down.astype(BF).reshape(2, 64, D)]
  transfers between devices with their start and end apart: 20 -> 6, of which waited for: 13 -> 6; matrix products, arithmetic and copies ran while one was open for 10% -> 0% of each run, Pallas kernels for 0% -> 0%
where the time goes in v1:
time: 677 us; the launch traced here: 667 us
  waiting for transfers between devices  307 us (45%)
  Pallas kernels  159 us (23%)
  local copies, waits for them, and re-layouts  61.5 us (9%)
  matrix products  58.6 us (9%)
  starting transfers between devices  40.9 us (6%)
  other arithmetic  23.1 us (3%)
  loops' own time  15.3 us (2%)
    ppermute x6, waiting for transfers between devices, relay(): return lax.ppermute(value, ('section', 'dp'), route)  307 us
    pallas_call x1, Pallas kernels, scatter(): pl.pallas_call(scatter_kernel, out_shape=[jax.ShapeDtypeStruct((2,) + tai...  82.1 us
    pallas_call x1, Pallas kernels, gather(): pl.pallas_call(gather_kernel, out_shape=[jax.ShapeDtypeStruct((4, 4, 2) +...  77 us
    ppermute x6, starting transfers between devices, relay(): return lax.ppermute(value, ('section', 'dp'), route)  40.9 us
    dot_general x6, matrix products, contract_rows(): lax.dot_general(left, right, (((0,), (0,)), ((), ())), preferred_element_...  18.6 us
    dot_general x6, matrix products, plain_dot(): return jnp.dot(left, right, preferred_element_type=F32)  18.5 us
    another operation x4, loops' own time, body(): lax.cond(role.x == tick, lambda ops: layer_backward(kept, ops[0], lengths...  14.9 us
    dot_general x6, matrix products, times_transpose(): lax.dot_general(left, right, (((1,), (1,)), ((), ())), preferred_element_...  14.7 us
  transfers between devices with their start and end apart: 6, of which 6 were waited for; matrix products, arithmetic and copies ran while one was open for 0% of the time, Pallas kernels for 0%

profile of v1, /device:TPU:1, one launch (start us, length us, event | category | flops | bytes accessed | tf_op | source)
XLA Modules:
  0.0 666.7 jit_solution(11814842197393221628)
XLA Ops:
  11.3 77.0 %gather_weights.1 = (bf16[4,4,2,2,16,2432]{5,4,3,2,1,0:T(8,128)(2,1)}, bf16[4,4,2,2,16,4096]{5,4,3,2,1,0:T(8,128)(2,1)}, bf16[4,4,2,2,64,1024]{5,4,3,2,1,0:T(8,128)(2,1)}, bf16[2,144,1024]{2,1,0:T(8,128)(2,1)}) custom-call(bf16[2,16,2432]{2,1,0:T(8,128)(2,1)} %copy-done.134, bf16[2,16,4096]{2,1,0:T(8,128)(2,1)} %bitcast.675, bf16[2,64,1024]{2,1,0:T(8,128)(2,1)} %bitcast.676, ...), custom_call_target="tpu_custom_call" | custom-call | tf_op jit(solution)/shard_map/gather_weights/pallas_call | solution.py:213
  93.1 4.0 fusion.225
  98.5 27.4 %conditional.8 = (bf16[256,1024]{1,0:T(8,128)(2,1)}, bf16[256,1024]{1,0:T(8,128)(2,1)S(1)}, bf16[256,1024]{1,0:T(8,128)(2,1)}, bf16[256,1024]{1,0:T(8,128)(2,1)}...) conditional(s32[]{:T(128)} %convert_element_type.491, ...), branch_computations={%region_0.1_spmd, %region_1.6_spmd} | conditional | flops 5649318912 | bytes 92671944 | solution.py:656
  112.3 8.7 %multiply_convert_fusion = (bf16[256,4096]{1,0:T(8,128)(2,1)}, f32[256,4096]{1,0:T(8,128)}) fusion(bf16[256,1024]{1,0:T(8,128)(2,1)S(1)} %multiply_convert_fusion.1, bf16[1024,4096]{1,0:T(8,128)(2,1)} %get-tuple-element.388), kind=kOutput, calls=%fused_computation.1 | convolution fusion | flops 2152726528 | bytes 15204352 | tf_op jit(solution)/shard_map/cond/branch_1_fun/dot_general | solution.py:500
  121.0 5.0 fusion.6
  127.6 11.7 %collective-permute-done = bf16[256,1024]{1,0:T(8,128)(2,1)S(1)} collective-permute-done((bf16[256,1024]{1,0:T(8,128)(2,1)}, bf16[256,1024]{1,0:T(8,128)(2,1)S(1)}, u32[]{:S(2)}, u32[]{:S(2)}) %collective-permute-start) | collective-permute-done | bytes 524320 | tf_op jit(solution)/shard_map/ppermute | solution.py:627
  139.3 31.3 %collective-permute-start.1 = (bf16[256,1024]{1,0:T(8,128)(2,1)S(1)}, bf16[256,1024]{1,0:T(8,128)(2,1)S(1)}, u32[]{:S(2)}, u32[]{:S(2)}) collective-permute-start(bf16[256,1024]{1,0:T(8,128)(2,1)S(1)} %get-tuple-element.603), channel_id=1, source_target_pairs={{0,1},{32,33},{2,3},{34,35},{4,5},{36,37},{6,7},{38,39},{8,9},{40,... | collective-permute-start | bytes 1572872 | tf_op jit(solution)/shard_map/ppermute | solution.py:627
  170.6 10.5 %collective-permute-done.1 = bf16[256,1024]{1,0:T(8,128)(2,1)S(1)} collective-permute-done((bf16[256,1024]{1,0:T(8,128)(2,1)S(1)}, bf16[256,1024]{1,0:T(8,128)(2,1)S(1)}, u32[]{:S(2)}, u32[]{:S(2)}) %collective-permute-start.1) | collective-permute-done | bytes 524320 | tf_op jit(solution)/shard_map/ppermute | solution.py:627
  181.9 4.1 collective-permute-start.2
  186.1 9.9 %collective-permute-done.2 = bf16[256,1024]{1,0:T(8,128)(2,1)S(1)} collective-permute-done((bf16[256,1024]{1,0:T(8,128)(2,1)}, bf16[256,1024]{1,0:T(8,128)(2,1)S(1)}, u32[]{:S(2)}, u32[]{:S(2)}) %collective-permute-start.2) | collective-permute-done | bytes 524320 | tf_op jit(solution)/shard_map/ppermute | solution.py:627
  197.0 15.1 %conditional.12 = (bf16[256,1024]{1,0:T(8,128)(2,1)}, bf16[4,4,2,2,16,2432]{5,4,3,2,1,0:T(8,128)(2,1)}, bf16[4,4,2,2,16,4096]{5,4,3,2,1,0:T(8,128)(2,1)}, bf16[4,4,2,2,64,1024]{5,4,3,2,1,0:T(8,128)(2,1)}) conditional(s32[]{:T(128)} %convert_element_type.494, bf16[256,1024]{1,0:T(8,128)(2,1)S(1)} %bitcast.616, (bf16[256,1024]{1,0:T(8,128)(2,1)S(1)}, ...), branch_computations={%region_24.25_spmd, %region_25.33_spmd} | conditional | flops 11308733440 | bytes 229732192 | solution.py:671
  200.7 4.4 broadcast_in_dim.90
  205.0 4.3 broadcast_in_dim.89
  213.5 37.1 %collective-permute-done.3 = bf16[256,1024]{1,0:T(8,128)(2,1)S(1)} collective-permute-done((bf16[256,1024]{1,0:T(8,128)(2,1)}, bf16[256,1024]{1,0:T(8,128)(2,1)S(1)}, u32[]{:S(2)}, u32[]{:S(2)}) %collective-permute-start.3) | collective-permute-done | bytes 524320 | tf_op jit(solution)/shard_map/ppermute | solution.py:627
  254.5 12.1 %collective-permute-done.4 = bf16[256,1024]{1,0:T(8,128)(2,1)S(1)} collective-permute-done((bf16[256,1024]{1,0:T(8,128)(2,1)S(1)}, bf16[256,1024]{1,0:T(8,128)(2,1)S(1)}, u32[]{:S(2)}, u32[]{:S(2)}) %collective-permute-start.4) | collective-permute-done | bytes 524320 | tf_op jit(solution)/shard_map/ppermute | solution.py:627
  266.6 8.9 %conditional.14 = (bf16[256,1024]{1,0:T(8,128)(2,1)S(1)}, bf16[4,4,2,2,16,2432]{5,4,3,2,1,0:T(8,128)(2,1)}, bf16[4,4,2,2,16,4096]{5,4,3,2,1,0:T(8,128)(2,1)}, bf16[4,4,2,2,64,1024]{5,4,3,2,1,0:T(8,128)(2,1)}) conditional(s32[]{:T(128)} %convert_element_type.492, (bf16[256,1024]{1,0:T(8,128)(2,1)S(1)}, bf16[4,4,2,2,16,2432]{5,4,3,2,1,0:T(8,128)(2,1)}, ...), branch_computations={%region_42.43_spmd, %region_43.51_spmd} | conditional | flops 11308733440 | bytes 231829376 | solution.py:671
  276.8 225.7 %collective-permute-done.5 = bf16[256,1024]{1,0:T(8,128)(2,1)} collective-permute-done((bf16[256,1024]{1,0:T(8,128)(2,1)S(1)}, bf16[256,1024]{1,0:T(8,128)(2,1)}, u32[]{:S(2)}, u32[]{:S(2)}) %collective-permute-start.5) | collective-permute-done | bytes 524320 | tf_op jit(solution)/shard_map/ppermute | solution.py:627
  502.5 70.4 %conditional.15 = (bf16[4,4,2,2,16,2432]{5,4,3,2,1,0:T(8,128)(2,1)}, bf16[4,4,2,2,16,4096]{5,4,3,2,1,0:T(8,128)(2,1)}, bf16[4,4,2,2,64,1024]{5,4,3,2,1,0:T(8,128)(2,1)}, bf16[2,128,1024]{2,1,0:T(8,128)(2,1)}) conditional(s32[]{:T(128)} %convert_element_type.491, (bf16[4,4,2,2,16,2432]{5,4,3,2,1,0:T(8,128)(2,1)}, ...), branch_computations={%region_51.52_spmd, %region_52.60_spmd} | conditional | flops 11308733440 | bytes 223436480 | solution.py:671
  503.2 7.7 %fusion.177 = bf16[256,4096]{1,0:T(8,128)(2,1)S(1)} fusion(bf16[4096,1024]{1,0:T(8,128)(2,1)} %get-tuple-element.487, f32[256,4096]{1,0:T(8,128)} %get-tuple-element.488, bf16[256,1024]{1,0:T(8,128)(2,1)} %get-tuple-element.484, f32[256]{0:T(256)S(1)} %fusion.206), kind=kOutput, calls=%fused_computation.347 | convolution fusion | flops 2157707264 | bytes 15205376 | tf_op jit(solution)/shard_map/cond/branch_1_fun/dot_general | solution.py:508
  513.1 3.8 multiply_reduce_fusion.16
  546.1 7.6 %convert_bitcast_fusion.7 = bf16[4096,1024]{0,1:T(8,128)(2,1)} fusion(bf16[256,4096]{1,0:T(8,128)(2,1)} %get-tuple-element.502, bf16[256,1024]{1,0:T(8,128)(2,1)} %get-tuple-element.484, f32[256]{0:T(256)S(1)} %fusion.206), kind=kOutput, calls=%fused_computation.343 | convolution fusion | flops 2152464384 | bytes 11011072 | tf_op jit(solution)/shard_map/cond/branch_1_fun/dot_general | solution.py:504
  554.9 12.1 %copy.173 = bf16[4096,1024]{1,0:T(8,128)(2,1)} copy(bf16[4096,1024]{0,1:T(8,128)(2,1)} %convert_bitcast_fusion.7) | data formatting | bytes 16777216 | tf_op jit(solution)/shard_map/cond/branch_1_fun/convert_element_type | solution.py:614
  567.0 5.6 convolution_convert_fusion.34
  572.9 82.1 %scatter_gradients.1 = (f32[2,16,2432]{2,1,0:T(8,128)}, f32[2,16,4096]{2,1,0:T(8,128)}, f32[2,64,1024]{2,1,0:T(8,128)}, bf16[2,32,1024]{2,1,0:T(8,128)(2,1)}, bf16[2,32,1024]{2,1,0:T(8,128)(2,1)}) custom-call(bf16[4,4,2,2,16,2432]{5,4,3,2,1,0:T(8,128)(2,1)} %get-tuple-element.650.g1, bf16[4,4,2,2,16,4096]{5,4,3,2,1,0:T(8,128)(2,1)} %get-tuple-element.651.g2, ...), custom_call_target="tpu_custom_call" | custom-call | tf_op jit(solution)/shard_map/scatter_gradients/pallas_call | solution.py:477
  (183 shorter events, 88.3 us)
Async XLA Ops:
  89.1 107.9 %copy-start.142 = (s32[2]{0:T(128)}, s32[2]{0:T(128)S(1)}, u32[]{:S(2)}) copy-start(s32[2]{0:T(128)S(1)} %convert_reduce_fusion) | copy-start | bytes 28
  90.2 7.2 %copy-start.33 = (bf16[2,128,1024]{2,1,0:T(8,128)(2,1)}, bf16[2,128,1024]{2,1,0:T(8,128)(2,1)S(1)}, u32[]{:S(2)}) copy-start(bf16[2,128,1024]{2,1,0:T(8,128)(2,1)S(1)} %slice.45) | copy-start | bytes 1572868
  102.0 4.7 copy-start.25
  102.3 4.7 copy-start.116
  102.6 4.5 copy-start.88
  106.3 4.4 copy-start.8
  107.1 13.8 %copy-start.66 = (bf16[32,8,8,128]{3,1,2,0:T(8,128)(2,1)}, bf16[32,8,8,128]{3,1,2,0:T(8,128)(2,1)S(1)}, u32[]{:S(2)}) copy-start(bf16[32,8,8,128]{3,1,2,0:T(8,128)(2,1)S(1)} %copy.338) | copy-start | bytes 1572868 | tf_op jit(solution)/shard_map/cond
  110.7 10.2 %slice-start = ((s8[8388608]{0:T(1024)(128)(4,1)}), s8[4194304]{0:T(1024)(128)(4,1)S(1)}, s32[]{:S(2)}) async-start(s8[8388608]{0:T(1024)(128)(4,1)} %bitcast.765), calls=%async_computation | async-start | bytes 8388608 | tf_op jit(solution)/shard_map/cond
  112.3 8.7 %copy-start.58 = (bf16[256,1024]{1,0:T(8,128)(2,1)}, bf16[256,1024]{1,0:T(8,128)(2,1)S(1)}, u32[]{:S(2)}) copy-start(bf16[256,1024]{1,0:T(8,128)(2,1)S(1)} %multiply_convert_fusion.1) | copy-start | bytes 1572868 | tf_op jit(solution)/shard_map/cond
  112.3 8.7 %slice-start.1 = ((s8[8388608]{0:T(1024)(128)(4,1)}), s8[4194304]{0:T(1024)(128)(4,1)S(1)}, s32[]{:S(2)}) async-start(s8[8388608]{0:T(1024)(128)(4,1)} %bitcast.765), calls=%async_computation.1 | async-start | bytes 8388608 | tf_op jit(solution)/shard_map/cond
  126.0 13.4 %collective-permute-start = (bf16[256,1024]{1,0:T(8,128)(2,1)}, bf16[256,1024]{1,0:T(8,128)(2,1)S(1)}, u32[]{:S(2)}, u32[]{:S(2)}) collective-permute-start(bf16[256,1024]{1,0:T(8,128)(2,1)} %get-tuple-element.591), channel_id=1, source_target_pairs={{0,1},{32,33},{2,3},{34,35},{4,5},{36,37},{6,7},{38,39},{8,9},{40,... | collective-permute-start | bytes 1572872 | tf_op jit(solution)/shard_map/ppermute | solution.py:627
  139.3 41.8 %collective-permute-start.1 = (bf16[256,1024]{1,0:T(8,128)(2,1)S(1)}, bf16[256,1024]{1,0:T(8,128)(2,1)S(1)}, u32[]{:S(2)}, u32[]{:S(2)}) collective-permute-start(bf16[256,1024]{1,0:T(8,128)(2,1)S(1)} %get-tuple-element.603), channel_id=1, source_target_pairs={{0,1},{32,33},{2,3},{34,35},{4,5},{36,37},{6,7},{38,39},{8,9},{40,... | collective-permute-start | bytes 1572872 | tf_op jit(solution)/shard_map/ppermute | solution.py:627
  181.9 14.0 %collective-permute-start.2 = (bf16[256,1024]{1,0:T(8,128)(2,1)}, bf16[256,1024]{1,0:T(8,128)(2,1)S(1)}, u32[]{:S(2)}, u32[]{:S(2)}) collective-permute-start(bf16[256,1024]{1,0:T(8,128)(2,1)} %copy-done.98), channel_id=1, source_target_pairs={{0,1},{32,33},{2,3},{34,35},{4,5},{36,37},{6,7},{38,39},{8,9},{40,... | collective-permute-start | bytes 1572872 | tf_op jit(solution)/shard_map/ppermute | solution.py:627
  212.2 38.4 %collective-permute-start.3 = (bf16[256,1024]{1,0:T(8,128)(2,1)}, bf16[256,1024]{1,0:T(8,128)(2,1)S(1)}, u32[]{:S(2)}, u32[]{:S(2)}) collective-permute-start(bf16[256,1024]{1,0:T(8,128)(2,1)} %get-tuple-element.638), channel_id=1, source_target_pairs={{1,0},{33,32},{3,2},{35,34},{5,4},{37,36},{7,6},{39,38},{9,8},{41,... | collective-permute-start | bytes 1572872 | tf_op jit(solution)/shard_map/ppermute | solution.py:627
  253.2 13.4 %collective-permute-start.4 = (bf16[256,1024]{1,0:T(8,128)(2,1)S(1)}, bf16[256,1024]{1,0:T(8,128)(2,1)S(1)}, u32[]{:S(2)}, u32[]{:S(2)}) collective-permute-start(bf16[256,1024]{1,0:T(8,128)(2,1)S(1)} %get-tuple-element.642), channel_id=1, source_target_pairs={{1,0},{33,32},{3,2},{35,34},{5,4},{37,36},{7,6},{39,38},{9,8},{41,... | collective-permute-start | bytes 1572872 | tf_op jit(solution)/shard_map/ppermute | solution.py:627
  275.5 227.0 %collective-permute-start.5 = (bf16[256,1024]{1,0:T(8,128)(2,1)S(1)}, bf16[256,1024]{1,0:T(8,128)(2,1)}, u32[]{:S(2)}, u32[]{:S(2)}) collective-permute-start(bf16[256,1024]{1,0:T(8,128)(2,1)S(1)} %get-tuple-element.649), channel_id=1, source_target_pairs={{1,0},{33,32},{3,2},{35,34},{5,4},{37,36},{7,6},{39,38},{9,8},{41,... | collective-permute-start | bytes 1572872 | tf_op jit(solution)/shard_map/ppermute | solution.py:627
  503.2 9.9 %copy-start.146 = (bf16[1024,4096]{1,0:T(8,128)(2,1)S(1)}, bf16[1024,4096]{1,0:T(8,128)(2,1)}, u32[]{:S(2)}) copy-start(bf16[1024,4096]{1,0:T(8,128)(2,1)} %get-tuple-element.489) | copy-start | bytes 25165828 | tf_op jit(solution)/shard_map/cond
  510.9 6.0 copy-start.104
  520.0 6.7 %copy-start.7 = (bf16[256,1024]{1,0:T(8,128)(2,1)S(1)}, bf16[256,1024]{1,0:T(8,128)(2,1)}, u32[]{:S(2)}) copy-start(bf16[256,1024]{1,0:T(8,128)(2,1)} %get-tuple-element.494) | copy-start | bytes 1572868 | tf_op jit(solution)/shard_map/cond
  520.4 12.8 %copy-start.123 = (bf16[256,128]{1,0:T(8,128)(2,1)S(1)}, bf16[256,128]{1,0:T(8,128)(2,1)}, u32[]{:S(2)}) copy-start(bf16[256,128]{1,0:T(8,128)(2,1)} %get-tuple-element.493) | copy-start | bytes 196612 | tf_op jit(solution)/shard_map/cond
  521.4 13.6 %copy-start.20 = (bf16[1024,1024]{1,0:T(8,128)(2,1)S(1)}, bf16[1024,1024]{1,0:T(8,128)(2,1)}, u32[]{:S(2)}) copy-start(bf16[1024,1024]{1,0:T(8,128)(2,1)} %get-tuple-element.496) | copy-start | bytes 6291460 | tf_op jit(solution)/shard_map/cond
  546.1 7.6 %copy-start.103 = (f32[256,1024]{1,0:T(8,128)S(1)}, f32[256,1024]{1,0:T(8,128)}, u32[]{:S(2)}) copy-start(f32[256,1024]{1,0:T(8,128)} %get-tuple-element.787) | copy-start | bytes 3145732 | tf_op jit(solution)/shard_map/cond
  554.9 12.1 %copy-start.65 = (bf16[256,1024]{1,0:T(8,128)(2,1)S(1)}, bf16[256,1024]{1,0:T(8,128)(2,1)}, u32[]{:S(2)}) copy-start(bf16[256,1024]{1,0:T(8,128)(2,1)} %get-tuple-element.501) | copy-start | bytes 1572868 | tf_op jit(solution)/shard_map/cond
  554.9 12.1 %copy-start.105 = (bf16[256,4096]{1,0:T(8,128)(2,1)S(1)}, bf16[256,4096]{1,0:T(8,128)(2,1)}, u32[]{:S(2)}) copy-start(bf16[256,4096]{1,0:T(8,128)(2,1)} %copy-done.104) | copy-start | bytes 6291460 | tf_op jit(solution)/shard_map/cond
  (23 other events, 54.9 us)

commit v2 on v0

v2 whole, which is shorter than its diff:
```python
import functools

import jax
import jax.numpy as jnp
from jax import lax
from jax.experimental import pallas as pl
from jax.experimental.pallas import tpu as pltpu
from jax.sharding import PartitionSpec as P

D = 1024
HEADS = 8
HD = 128
FF = 4096
LAYERS = 4
SEQ = 128
MICRO = 2
NORM_EPS = 1e-06
NEG_FILL = -1000000000.0
W1 = D + 2 * HD + HD + D
BF = jnp.bfloat16
F32 = jnp.float32
MESH = pl.DeviceIdType.MESH


class Role:
    def __init__(self):
        section = lax.axis_index("section")
        dp = lax.axis_index("dp")
        self.c = section % 2
        self.x_lo = dp % 2
        self.x = (section // 2) * 2 + self.x_lo
        self.z = (dp // 2) % 4
        self.y = dp // 8
        self.native = self.c == self.x_lo

    def dev(self, x, y, z, c):
        return ((x // 2) * 2 + c, (y * 4 + z) * 2 + x % 2)

    def along(self, axis, step):
        if axis == 0:
            return self.dev(self.x, (self.y + step + 4) % 4, self.z, self.c)
        return self.dev(self.x, self.y, (self.z + step + 4) % 4, self.c)

    def partner(self):
        return self.dev(self.x, self.y, self.z, 1 - self.c)

    def swap(self):
        return self.dev(self.x + 1 - 2 * self.x_lo, self.y, self.z, 1 - self.c)


def remote(src, dst, sems, device):
    return pltpu.make_async_remote_copy(
        src_ref=src, dst_ref=dst, send_sem=sems[0], recv_sem=sems[1], device_id=device, device_id_type=MESH
    )


def greet(devices):
    barrier = pltpu.get_barrier_semaphore()
    for device in devices:
        pl.semaphore_signal(barrier, inc=1, device_id=device, device_id_type=MESH)
    pl.semaphore_wait(barrier, len(devices))


class Bufs:
    pass


SCRATCH = (
    ("w1", (4, 4, 2, 2, 16, W1), BF),
    ("w2", (4, 4, 2, 2, 16, FF), BF),
    ("w3", (4, 4, 2, 2, 64, D), BF),
    ("g1", (4, 4, 2, 2, 16, W1), BF),
    ("g2", (4, 4, 2, 2, 16, FF), BF),
    ("g3", (4, 4, 2, 2, 64, D), BF),
    ("act", (MICRO, SEQ + 16, D), BF),
    ("hb", (MICRO, SEQ, D), BF),
    ("gb", (MICRO, SEQ, D), BF),
    ("ho", (MICRO, SEQ, D), BF),
    ("xa", (MICRO, SEQ, D), BF),
    ("qkv", (MICRO, SEQ, D + 2 * HD), BF),
    ("probs", (MICRO, HEADS * SEQ, SEQ), F32),
    ("mixed", (MICRO, SEQ, D), BF),
    ("after", (MICRO, SEQ, D), F32),
    ("xf", (MICRO, SEQ, D), BF),
    ("u", (MICRO, SEQ, FF), BF),
    ("dp", (MICRO, SEQ, FF), BF),
    ("gf", (MICRO, SEQ, D), BF),
    ("dx", (SEQ, D), F32),
    ("dr", (SEQ, D), F32),
    ("ga", (MICRO, SEQ, D), BF),
    ("do", (SEQ, D), BF),
    ("dqkv", (MICRO, SEQ, D + 2 * HD), BF),
    ("gains", (8, D), F32),
    ("gain_sums", (2, MICRO, 8, D), F32),
)


def dot(left, right):
    return jnp.dot(left, right, preferred_element_type=F32)


def dot_nt(left, right):
    return lax.dot_general(left, right, (((1,), (1,)), ((), ())), preferred_element_type=F32)


def dot_tn(left, right):
    return lax.dot_general(left, right, (((0,), (0,)), ((), ())), preferred_element_type=F32)


def rms_factor(values):
    return lax.rsqrt(jnp.mean(values * values, axis=-1, keepdims=True) + NORM_EPS)


def norm_back(grad_normed, normed, factor):
    return factor * (grad_normed - normed * jnp.mean(grad_normed * normed, axis=-1, keepdims=True))


def tile(at, wide):
    return pl.ds(pl.multiple_of(at * wide, wide), wide)


def heads_down(value):
    return jnp.concatenate([value[:, h * HD : (h + 1) * HD] for h in range(HEADS)], axis=0)


def heads_across(value):
    return jnp.concatenate([value[h * SEQ : (h + 1) * SEQ] for h in range(HEADS)], axis=1)


def pad_column(act, m):
    length = act[m, SEQ : SEQ + 1, 0:1].astype(F32)
    positions = lax.broadcasted_iota(jnp.int32, (SEQ, 1), 0).astype(F32)
    return jnp.where(positions < length, 1.0, 0.0)


def read_gains(b):
    for start in range(4):
        block = b.w1[start, :, :, :, :, D + 2 * HD : D + 3 * HD].reshape(D // 4, HD).astype(F32)
        b.gains[:, start * 256 : (start + 1) * 256] = jnp.transpose(block)[0:8]


def forward_layer(b, m):
    pad = pad_column(b.act, m)
    hidden = b.hb[m].astype(F32)
    b.xa[m] = (hidden * rms_factor(hidden) * b.gains[0:1, :]).astype(BF)

    @pl.loop(0, (D + 2 * HD) // 256)
    def _(n):
        b.qkv[m, :, tile(n, 256)] = dot(b.xa[m], b.w1[:, :, :, :, :, tile(n, 256)].reshape(D, 256)).astype(BF)

    length = b.act[m, SEQ : SEQ + 1, 0:1].astype(F32)
    rows = lax.broadcasted_iota(jnp.int32, (SEQ, SEQ), 0)
    columns = lax.broadcasted_iota(jnp.int32, (SEQ, SEQ), 1)
    allowed = jnp.logical_and(columns <= rows, columns.astype(F32) < length)
    keys_all = b.qkv[m, :, D : D + HD]
    values_all = b.qkv[m, :, D + HD : D + 2 * HD]
    scores = dot_nt(heads_down(b.qkv[m, :, 0:D]), keys_all) * HD ** (-0.5)
    scores = jnp.where(allowed[None], scores.reshape(HEADS, SEQ, SEQ), NEG_FILL)
    raised = jnp.exp(scores - jnp.max(scores, axis=-1, keepdims=True))
    probs = (raised / jnp.sum(raised, axis=-1, keepdims=True)).reshape(HEADS * SEQ, SEQ)
    b.probs[m] = probs
    b.mixed[m] = heads_across(dot(probs.astype(BF), values_all)).astype(BF)

    @pl.loop(0, D // 256)
    def _(n):
        w = b.w1[:, :, :, :, :, pl.ds(pl.multiple_of(W1 - D + n * 256, HD), 256)].reshape(D, 256)
        b.after[m, :, tile(n, 256)] = b.hb[m, :, tile(n, 256)].astype(F32) + pad * dot(b.mixed[m], w)

    after = b.after[m]
    b.xf[m] = (after * rms_factor(after) * b.gains[1:2, :]).astype(BF)

    @pl.loop(0, FF // 512)
    def _(n):
        a = dot(b.xf[m], b.w2[:, :, :, :, :, tile(n, 512)].reshape(D, 512))
        sigmoid = 1.0 / (1.0 + jnp.exp(-a))
        b.u[m, :, tile(n, 512)] = (a * sigmoid).astype(BF)
        b.dp[m, :, tile(n, 512)] = (sigmoid * (1.0 + a * (1.0 - sigmoid))).astype(BF)

    @pl.loop(0, D // 256)
    def _(n):
        w = b.w3[:, :, :, :, :, tile(n, 256)].reshape(FF, 256)
        b.ho[m, :, tile(n, 256)] = (b.after[m, :, tile(n, 256)] + pad * dot(b.u[m], w)).astype(BF)


def backward_ffn(b, m):
    pad = pad_column(b.act, m)
    b.gf[m] = (b.gb[m].astype(F32) * pad).astype(BF)

    @pl.loop(0, 16)
    def _(n):
        w = b.w3[n // 4, n % 4].reshape(256, D)
        b.dp[m, :, tile(n, 256)] = (dot_nt(b.gf[m], w) * b.dp[m, :, tile(n, 256)].astype(F32)).astype(BF)

    @pl.loop(0, 4)
    def _(n):
        b.dx[:, tile(n, 256)] = dot_nt(b.dp[m], b.w2[n].reshape(256, FF))

    after = b.after[m]
    factor = rms_factor(after)
    normed = after * factor
    d_xf = b.dx[...]
    b.gain_sums[1, m] = jnp.sum((d_xf * normed).reshape(SEQ // 8, 8, D), axis=0)
    d_r = b.gb[m].astype(F32) + norm_back(d_xf * b.gains[1:2, :], normed, factor)
    b.dr[...] = d_r
    b.ga[m] = (d_r * pad).astype(BF)


def backward_attention(b, m):
    scale = HD ** (-0.5)

    @pl.loop(0, 4)
    def _(n):
        b.do[:, tile(n, 256)] = dot_nt(b.ga[m], b.w1[n, :, :, :, :, W1 - D :].reshape(256, D)).astype(BF)

    d_mixed = heads_down(b.do[...])
    keys_all = b.qkv[m, :, D : D + HD]
    values_all = b.qkv[m, :, D + HD : D + 2 * HD]
    probs = b.probs[m]
    d_p = dot_nt(d_mixed, values_all)
    b.dqkv[m, :, D + HD : D + 2 * HD] = dot_tn(probs.astype(BF), d_mixed).astype(BF)
    d_s = (probs * (d_p - jnp.sum(probs * d_p, axis=-1, keepdims=True))).astype(BF)
    b.dqkv[m, :, 0:D] = heads_across(dot(d_s, keys_all) * scale).astype(BF)
    b.dqkv[m, :, D : D + HD] = (dot_tn(d_s, heads_down(b.qkv[m, :, 0:D])) * scale).astype(BF)

    @pl.loop(0, 4)
    def _(n):
        w = b.w1[n, :, :, :, :, 0 : D + 2 * HD].reshape(256, D + 2 * HD)
        b.dx[:, tile(n, 256)] = dot_nt(b.dqkv[m], w)

    hidden = b.hb[m].astype(F32)
    factor = rms_factor(hidden)
    normed = hidden * factor
    d_xa = b.dx[...]
    b.gain_sums[0, m] = jnp.sum((d_xa * normed).reshape(SEQ // 8, 8, D), axis=0)
    b.ho[m] = (b.dr[...] + norm_back(d_xa * b.gains[0:1, :], normed, factor)).astype(BF)


def both(ref, cols):
    return ref[:, :, cols].reshape(MICRO * SEQ, -1)


def grads_down(b):
    @pl.loop(0, 16)
    def _(n):
        left = b.u[:, :, tile(n, 256)].reshape(MICRO * SEQ, 256)
        b.g3[n // 4, n % 4] = dot_tn(left, b.gf[...].reshape(MICRO * SEQ, D)).astype(BF).reshape(2, 2, 64, D)


def grads_up(b):
    @pl.loop(0, 16)
    def _(n):
        left = b.xf[:, :, tile(n // 4, 256)].reshape(MICRO * SEQ, 256)
        right = b.dp[:, :, tile(n % 4, D)].reshape(MICRO * SEQ, D)
        b.g2[n // 4, :, :, :, :, tile(n % 4, D)] = dot_tn(left, right).astype(BF).reshape(4, 2, 2, 16, D)


def grads_first(b):
    wide = D + 2 * HD

    @pl.loop(0, 4)
    def _(n):
        left = b.xa[:, :, tile(n, 256)].reshape(MICRO * SEQ, 256)
        b.g1[n, :, :, :, :, 0:wide] = dot_tn(left, b.dqkv[...].reshape(MICRO * SEQ, wide)).astype(BF).reshape(4, 2, 2, 16, wide)
        left = b.mixed[:, :, tile(n, 256)].reshape(MICRO * SEQ, 256)
        b.g1[n, :, :, :, :, W1 - D :] = dot_tn(left, b.ga[...].reshape(MICRO * SEQ, D)).astype(BF).reshape(4, 2, 2, 16, D)

    lines = [jnp.sum(b.gain_sums[k, 0] + b.gain_sums[k, 1], axis=0, keepdims=True) for k in range(2)]
    sums = jnp.concatenate(lines + [jnp.zeros((HD - 2, D), F32)], axis=0)
    for n in range(4):
        block = jnp.transpose(sums[:, n * 256 : (n + 1) * 256]).astype(BF)
        b.g1[n, :, :, :, :, D + 2 * HD : D + 3 * HD] = block.reshape(4, 2, 2, 16, HD)


N_GATHER = 12
N_SCATTER = 9
GATHER_CUTS = ((0, 1), (1, 2), (2, 2))
SCATTER_CUTS = ((2, 2), (1, 2), (0, 1))
STEPS = 5
WIDTHS = (W1, FF, D)
SEMAPHORES = (
    ("ag_send", STEPS * 2 * N_GATHER),
    ("ag_recv", STEPS * 2 * N_GATHER),
    ("ag_swap_send", STEPS + 1),
    ("ag_swap_recv", STEPS + 1),
    ("ag_local", STEPS + 1),
    ("rs_send", STEPS * 2 * N_SCATTER),
    ("rs_recv", STEPS * 2 * N_SCATTER),
    ("rs_swap_send", STEPS * 2),
    ("rs_swap_recv", STEPS * 2),
    ("relay_send", 2 * MICRO),
    ("relay_recv", 2 * MICRO),
    ("row_send", 2 * MICRO * LAYERS),
    ("row_recv", 2 * MICRO),
    ("row_local", 2 * MICRO),
)


def cut(cuts):
    made = []
    for which, count in cuts:
        wide = WIDTHS[which] // count
        for at in range(count):
            made.append((which, at * wide, wide))
    return made


def near_far(chunk, part):
    which, start, wide = chunk
    near = (wide // HD + 1) // 2 * HD
    return pl.ds(start, near) if part == 0 else pl.ds(start + near, wide - near)


def gather_weights(role, shards, fulls, act_in, b, sem):
    y, z, c = role.y, role.z, role.c
    place = (y, z)
    chunks = cut(GATHER_CUTS)
    count = len(chunks)

    def own_copies(step, owner):
        which, start, wide = chunks[step]
        src = shards[which].at[:, :, pl.ds(start, wide)]
        dst = fulls[which].at[y, z, owner, :, :, pl.ds(start, wide)]
        return (
            remote(src, dst, (sem.ag_swap_send.at[step], sem.ag_swap_recv.at[step]), role.swap()),
            pltpu.make_async_copy(src, dst, sem.ag_local.at[step]),
        )

    act_far = remote(act_in, b.act, (sem.ag_swap_send.at[count], sem.ag_swap_recv.at[count]), role.swap())
    act_near = pltpu.make_async_copy(act_in, b.act, sem.ag_local.at[count])

    @pl.when(role.native)
    def _():
        for step in range(count):
            own_copies(step, c)[1].start()
        act_near.start()

    @pl.when(jnp.logical_not(role.native))
    def _():
        for step in range(count):
            own_copies(step, 1 - c)[0].start()
        act_far.start()

    def piece(step, half, first, second, part=None):
        which, start, wide = chunks[step]
        cols = pl.ds(start, wide) if part is None else near_far(chunks[step], part)
        index = (first, second) if half == 0 else (second, first)
        return fulls[which].at[index[0], index[1], c, half, :, cols]

    def hop(step, half, number):
        one, two = half, 1 - half
        p, s = place[one], place[two]
        nxt, prv = (p + 1) % 4, (p + 3) % 4
        snx, spv, sop = (s + 1) % 4, (s + 3) % 4, (s + 2) % 4
        every, low, high = slice(None), pl.ds(0, 2), pl.ds(2, 2)
        first, second, part, device = (
            (p, s, None, role.along(one, 1)),
            (p, s, None, role.along(one, -1)),
            (prv, s, 0, role.along(one, 1)),
            (nxt, s, 1, role.along(one, -1)),
            (every, s, None, role.along(two, 1)),
            (every, s, None, role.along(two, -1)),
            (low, spv, None, role.along(two, 1)),
            (high, snx, None, role.along(two, -1)),
            (every, s, None, role.partner()),
            (every, spv, None, role.partner()),
            (every, snx, None, role.partner()),
            (every, sop, None, role.partner()),
        )[number]
        view = piece(step, half, first, second, part)
        at = (step * 2 + half) * N_GATHER + number
        return remote(view, view, (sem.ag_send.at[at], sem.ag_recv.at[at]), device)

    arrive = ((), (0, 1), (2, 3), (4, 5), (6, 7))
    leave = ((0, 1), (2, 3), (4, 5, 8), (6, 7, 9, 10), (11,))
    for tick in range(count + 4):
        for level in range(5):
            step = tick - level
            if not 0 <= step < count:
                continue
            if level == 0:

                @pl.when(role.native)
                def _():
                    own_copies(step, c)[1].wait()

                @pl.when(jnp.logical_not(role.native))
                def _():
                    own_copies(step, 1 - c)[0].wait()

            for half in (0, 1):
                for number in arrive[level]:
                    hop(step, half, number).wait_recv()
                for number in leave[level]:
                    hop(step, half, number).start()
    for step in range(count):
        for half in (0, 1):
            for number in (8, 9, 10, 11):
                hop(step, half, number).wait_recv()
            for number in range(N_GATHER):
                hop(step, half, number).wait_send()

    @pl.when(role.native)
    def _():
        act_near.wait()

    @pl.when(jnp.logical_not(role.native))
    def _():
        act_far.wait()


class Scatter:
    def __init__(self, role, grads, works, swaps, outs, sem, free):
        self.role, self.grads, self.works, self.swaps, self.outs = role, grads, works, swaps, outs
        self.sem, self.free = sem, free
        self.chunks = cut(SCATTER_CUTS)
        self.peers = [role.along(0, 1), role.along(0, -1), role.along(1, 1), role.along(1, -1), role.partner()]

    def say_free(self, which):
        for device in self.peers:
            pl.semaphore_signal(self.free.at[which], inc=1, device_id=device, device_id_type=MESH)

    def wait_free(self, which):
        pl.semaphore_wait(self.free.at[which], len(self.peers))

    def cols(self, step):
        which, start, wide = self.chunks[step]
        return pl.ds(start, wide)

    def core_copy(self, step):
        which = self.chunks[step][0]
        at = step * 2 * N_SCATTER
        return remote(
            self.grads[which].at[:, :, 1 - self.role.c, :, :, self.cols(step)],
            self.works[which].at[:, :, 0, :, :, self.cols(step)],
            (self.sem.rs_send.at[at], self.sem.rs_recv.at[at]),
            self.role.partner(),
        )

    def piece(self, step, half, first, second, part=None):
        index = (first, second) if half == 0 else (second, first)
        cols = self.cols(step) if part is None else near_far(self.chunks[step], part)
        return self.grads[self.chunks[step][0]].at[index[0], index[1], self.role.c, half, :, cols]

    def spot(self, step, half, first, second, part=None):
        cols = self.cols(step) if part is None else near_far(self.chunks[step], part)
        return self.works[self.chunks[step][0]].at[first, second, 1, half, :, cols]

    def hop(self, step, half, number):
        role = self.role
        place = (role.y, role.z)
        one, two = half, 1 - half
        p, s = place[one], place[two]
        nxt, prv, opp = (p + 1) % 4, (p + 3) % 4, (p + 2) % 4
        snx, spv, sop = (s + 1) % 4, (s + 3) % 4, (s + 2) % 4
        every, low, high = slice(None), pl.ds(0, 2), pl.ds(2, 2)
        src, dst = (
            ((opp, low, None), (2, low, None)),
            ((opp, high, None), (2, high, None)),
            ((nxt, every, None), (0, every, None)),
            ((prv, every, None), (1, every, None)),
            ((p, sop, 0), (3, 0, 0)),
            ((p, sop, 1), (3, 1, 1)),
            ((p, snx, None), (3, 2, None)),
            ((p, spv, None), (3, 3, None)),
        )[number]
        axis = one if number < 4 else two
        at = (step * 2 + half) * N_SCATTER + 1 + number
        return remote(
            self.piece(step, half, *src),
            self.spot(step, half, *dst),
            (self.sem.rs_send.at[at], self.sem.rs_recv.at[at]),
            role.along(axis, 1 if number % 2 == 0 else -1),
        )

    def swapped(self, step, half):
        which = self.chunks[step][0]
        at = step * 2 + half
        return remote(
            self.grads[which].at[self.role.y, self.role.z, self.role.c, half, :, self.cols(step)],
            self.swaps[which].at[half, :, self.cols(step)],
            (self.sem.rs_swap_send.at[at], self.sem.rs_swap_recv.at[at]),
            self.role.swap(),
        )

    def add_core(self, step):
        self.core_copy(step).wait_recv()
        which = self.chunks[step][0]
        cols, c = self.cols(step), self.role.c
        grad, work = self.grads[which], self.works[which]

        @pl.loop(0, 16)
        def _(at):
            y, z = at // 4, at % 4
            grad[y, z, c, :, :, cols] = grad[y, z, c, :, :, cols] + work[y, z, 0, :, :, cols]

    def level(self, step, half, number):
        role = self.role
        place = (role.y, role.z)
        one, two = half, 1 - half
        p, s = place[one], place[two]
        nxt, prv = (p + 1) % 4, (p + 3) % 4
        snx, spv = (s + 1) % 4, (s + 3) % 4
        which = self.chunks[step][0]
        if number > 0:
            self.hop(step, half, 2 * number - 2).wait_recv()
            self.hop(step, half, 2 * number - 1).wait_recv()

        def add(there, *spots):
            total = there[...].astype(F32)
            for spot in spots:
                total = total + spot[...].astype(F32)
            there[...] = total.astype(BF)

        if number == 1:
            for i in range(2):
                add(self.piece(step, half, nxt, i), self.spot(step, half, 2, i))
                add(self.piece(step, half, prv, 2 + i), self.spot(step, half, 2, 2 + i))
        elif number == 2:
            for i in range(4):
                add(self.piece(step, half, p, i), self.spot(step, half, 0, i), self.spot(step, half, 1, i))
        elif number == 3:
            add(self.piece(step, half, p, snx, 0), self.spot(step, half, 3, 0, 0))
            add(self.piece(step, half, p, spv, 1), self.spot(step, half, 3, 1, 1))
        elif number == 4:
            here = self.piece(step, half, p, s)
            total = here[...].astype(F32)
            for i in (2, 3):
                total = total + self.spot(step, half, 3, i)[...].astype(F32)

            @pl.when(role.native)
            def _():
                self.outs[which][half, :, self.cols(step)] = total

            @pl.when(jnp.logical_not(role.native))
            def _():
                here[...] = total.astype(BF)
                self.swapped(step, half).start()

        if number < 4:
            self.hop(step, half, 2 * number).start()
            self.hop(step, half, 2 * number + 1).start()

    def run(self):
        count = len(self.chunks)
        for step in range(count):
            which = self.chunks[step][0]
            if step == 0 or self.chunks[step - 1][0] != which:
                self.wait_free(which)
            self.core_copy(step).start()
        for tick in range(count + 4):
            for number in range(4, -1, -1):
                step = tick - number
                if 0 <= step < count:
                    if number == 0:
                        self.add_core(step)
                    for half in (0, 1):
                        self.level(step, half, number)

    def finish(self):
        role = self.role

        @pl.when(jnp.logical_not(role.native))
        def _():
            for step in range(len(self.chunks)):
                which = self.chunks[step][0]
                for half in (0, 1):
                    self.swapped(step, half).wait()
                    self.outs[which][half, :, self.cols(step)] = self.swaps[which][half, :, self.cols(step)].astype(F32)

        for step in range(len(self.chunks)):
            self.core_copy(step).wait_send()
            for half in (0, 1):
                for number in range(8):
                    self.hop(step, half, number).wait_send()


class Rows:
    def __init__(self, role, which, source, out, sem):
        self.role, self.which, self.source, self.out, self.sem = role, which, source, out, sem
        self.source_x = (3, 0)[which]
        self.holds = role.x == self.source_x

    def copies(self, m):
        role, rows = self.role, SEQ // LAYERS
        made = []
        for section in range(LAYERS):
            target_x, target_c = 2 * (section // 2) + role.c, section % 2
            src = self.source.at[m, pl.ds(section * rows, rows)]
            at = (self.which * MICRO + m) * LAYERS + section
            arrival = self.which * MICRO + m
            here = jnp.logical_and(target_x == self.source_x, target_c == role.c)
            far = remote(
                src, self.out.at[m], (self.sem.row_send.at[at], self.sem.row_recv.at[arrival]), role.dev(target_x, role.y, role.z, target_c)
            )
            near = pltpu.make_async_copy(src, self.out.at[m], self.sem.row_local.at[arrival])
            made.append((here, far, near))
        return made

    def start(self, m):
        @pl.when(self.holds)
        def _():
            for here, far, near in self.copies(m):
                pl.when(here)(near.start)
                pl.when(jnp.logical_not(here))(far.start)

    def sent(self, m):
        @pl.when(self.holds)
        def _():
            for here, far, near in self.copies(m):
                pl.when(here)(near.wait)
                pl.when(jnp.logical_not(here))(far.wait_send)

    def arrived(self, m):
        kept = jnp.logical_and(self.holds, (self.role.x // 2) * 2 + self.role.c == self.role.x)
        kept = jnp.logical_and(kept, self.role.x_lo == self.role.c)

        @pl.when(jnp.logical_not(kept))
        def _():
            self.copies(m)[0][1].wait_recv()


def decoder_kernel(*refs):
    names = [name for name, _, _ in SCRATCH]
    s1, s2, s3, act_in, o1, o2, o3, final_out, start_out = refs[:9]
    b, sem = Bufs(), Bufs()
    rest = list(refs[9:])
    for name in names:
        setattr(b, name, rest.pop(0))
    swaps = [rest.pop(0) for _ in range(3)]
    for name, _ in SEMAPHORES:
        setattr(sem, name, rest.pop(0))
    free = rest.pop(0)

    role = Role()
    x, y, z, c = role.x, role.y, role.z, role.c
    peers = [role.along(0, 1), role.along(0, -1), role.along(1, 1), role.along(1, -1)]
    for away in range(4):
        for other in range(2):
            if (away, other) != (0, 0):
                peers.append(role.dev((x + away) % 4, y, z, (c + other) % 2))
    greet(peers)

    gather_weights(role, (s1, s2, s3), (b.w1, b.w2, b.w3), act_in, b, sem)
    read_gains(b)
    first, last = x == 0, x == LAYERS - 1

    @pl.when(first)
    def _():
        b.hb[...] = b.act[:, 0:SEQ]

    @pl.when(last)
    def _():
        b.gb[...] = b.act[:, 0:SEQ]

    def relay(which, m):
        dst, there = ((b.hb, (x + 1) % 4), (b.gb, (x + 3) % 4))[which]
        at = which * MICRO + m
        return remote(b.ho.at[m], dst.at[m], (sem.relay_send.at[at], sem.relay_recv.at[at]), role.dev(there, y, z, c))

    final_rows = Rows(role, 0, b.ho, final_out, sem)
    start_rows = Rows(role, 1, b.ho, start_out, sem)

    @pl.loop(0, MICRO)
    def _(m):
        pl.when(jnp.logical_not(first))(lambda: relay(0, m).wait_recv())
        forward_layer(b, m)
        pl.when(jnp.logical_not(last))(lambda: relay(0, m).start())
        final_rows.start(m)

    scatter = Scatter(role, (b.g1, b.g2, b.g3), (b.w1, b.w2, b.w3), swaps, (o1, o2, o3), sem, free)

    @pl.loop(0, MICRO)
    def _(m):
        pl.when(jnp.logical_not(last))(lambda: relay(1, m).wait_recv())
        backward_ffn(b, m)
        pl.when(jnp.logical_not(last))(lambda: relay(0, m).wait_send())
        final_rows.sent(m)
        backward_attention(b, m)
        pl.when(jnp.logical_not(first))(lambda: relay(1, m).start())
        start_rows.start(m)

    for which in (2, 1, 0):
        scatter.say_free(which)
    grads_down(b)
    grads_up(b)
    grads_first(b)
    scatter.run()
    scatter.finish()
    for m in range(MICRO):
        pl.when(jnp.logical_not(first))(lambda: relay(1, m).wait_send())
        start_rows.sent(m)
        final_rows.arrived(m)
        start_rows.arrived(m)


def decoder(s1, s2, s3, act):
    hbm = pl.BlockSpec(memory_space=pl.ANY)
    vmem = pl.BlockSpec(memory_space=pltpu.VMEM)
    shapes = [s.shape for s in (s1, s2, s3)]
    rows = SEQ // LAYERS
    return pl.pallas_call(
        decoder_kernel,
        out_shape=[jax.ShapeDtypeStruct(shape, F32) for shape in shapes]
        + [jax.ShapeDtypeStruct((MICRO, rows, D), BF)] * 2,
        in_specs=[hbm] * 4,
        out_specs=[vmem] * 3 + [hbm] * 2,
        scratch_shapes=[pltpu.VMEM(shape, dtype) for _, shape, dtype in SCRATCH]
        + [pltpu.VMEM(shape, BF) for shape in shapes]
        + [pltpu.SemaphoreType.DMA((count,)) for _, count in SEMAPHORES]
        + [pltpu.SemaphoreType.REGULAR((3,))],
        compiler_params=pltpu.CompilerParams(collective_id=0, has_side_effects=True, vmem_limit_bytes=63 << 20),
        name="decoder_step",
    )(s1, s2, s3, act)


def body(
    inputs, cotangent, lengths, attn_gain, w_query, w_key, w_value, w_out, ffn_gain, w_up, w_down
):
    role = Role()
    gains = jnp.pad(jnp.stack([attn_gain, ffn_gain], axis=1), ((0, 0), (0, HD - 2)))
    first = jnp.concatenate([w_query, w_key, w_value, gains, w_out], axis=1).astype(BF).reshape(2, 16, W1)
    second = w_up.astype(BF).reshape(2, 16, FF)
    third = w_down.astype(BF).reshape(2, 64, D)
    rows = jnp.where(role.x < 2, inputs[:, 0], cotangent[:, 0])
    lengths_rows = jnp.broadcast_to(lengths.astype(BF)[:, :, None], (MICRO, 16, D))
    act = jnp.concatenate([rows, lengths_rows], axis=1)
    o1, o2, o3, final_rows, input_rows = decoder(first, second, third, act)
    o1 = o1.reshape(32, W1)
    return (
        final_rows[:, None],
        input_rows[:, None],
        o1[:, D + 2 * HD],
        o1[:, :D],
        o1[:, D : D + HD],
        o1[:, D + HD : D + 2 * HD],
        o1[:, W1 - D :],
        o1[:, D + 2 * HD + 1],
        o2.reshape(32, FF),
        o3.reshape(128, D),
    )


def solution(mesh):
    both_axes = P(("section", "dp"))
    both_rows = P(("section", "dp"), None)
    acts = P(None, "dp", None, None)
    outs = P(None, "dp", "section", None)
    weights = (both_axes, both_rows, both_rows, both_rows, both_rows, both_axes, both_rows, both_rows)
    return jax.shard_map(
        body,
        mesh=mesh,
        in_specs=(acts, acts, P(None, "dp")) + weights,
        out_specs=(outs, outs) + weights,
        check_vma=False,
    )
```

time: 2300 us -> 314 us (0.14); the launches traced: 2270 us -> 313 us
  waiting for transfers between devices: 1390 us -> 0 us
  Pallas kernels: 0 us -> 296 us
  blocking collectives: 274 us -> 0 us
  other arithmetic: 208 us -> 7.04 us
  local copies, waits for them, and re-layouts: 199 us -> 9.4 us
  matrix products: 125 us -> 0 us
  starting transfers between devices: 40.3 us -> 0 us
    reduce_scatter x6 -> x0, waiting for transfers between devices: 829 us -> none  [the longest x1 200 us: body(): lax.psum_scatter(totals[6].astype(jnp.bfloat16), 'dp', scatter_dimension=...]
    all_gather x4 -> x0, waiting for transfers between devices: 489 us -> none  [the longest x1 213 us: body(): lax.all_gather(w_up.astype(jnp.bfloat16), 'dp', axis=0, tiled=True)]
    pallas_call x0 -> x1, Pallas kernels: none -> 296 us  [decoder(): pl.pallas_call(decoder_kernel, out_shape=[jax.ShapeDtypeStruct(shape, F32...]
    unnamed x2 -> x0, blocking collectives: 140 us -> none
    all_gather x2 -> x0, blocking collectives: 134 us -> none  [the longest x1 68 us: body(): lax.all_gather(w_key.astype(jnp.bfloat16), 'dp', axis=0, tiled=True)]
    dot_general x46 -> x0, matrix products: 120 us -> none  [the longest x12 53.5 us: contract_rows(): lax.dot_general(left_side, right_side, (((0,), (0,)), ((), ())), preferre...]
    convert_element_type x44 -> x2, other arithmetic: 121 us -> 1.47 us  [the longest x1 0.74 us: body(): third = w_down.astype(BF).reshape(2, 64, D)]
    another operation x90 -> x0, local copies, waits for them, and re-layouts: 111 us -> none
  transfers between devices with their start and end apart: 20 -> 0, of which waited for: 13 -> 0; matrix products, arithmetic and copies ran while one was open for 10% -> 0% of each run, Pallas kernels for 0% -> 0%
where the time goes in v2:
time: 314 us; the launch traced here: 313 us
  Pallas kernels  296 us (94%)
  local copies, waits for them, and re-layouts  9.4 us (3%)
  other arithmetic  7.04 us (2%)
    pallas_call x1, Pallas kernels, decoder(): pl.pallas_call(decoder_kernel, out_shape=[jax.ShapeDtypeStruct(shape, F32...  296 us

profile of v2, /device:TPU:1, one launch (start us, length us, event | category | flops | bytes accessed | tf_op | source)
XLA Modules:
  0.0 313.4 jit_solution(16884881956199498084)
XLA Ops:
  0.7 0.7 convert_bitcast_fusion
  1.4 0.7 convert_bitcast_fusion.1
  2.1 0.1 copy.31
  2.2 0.7 convert.29
  2.9 0.7 convert.30
  3.6 0.1 broadcast_in_dim.15
  3.7 0.9 convert.28
  4.6 0.9 convert.33
  5.6 0.0 copy-start.3
  5.6 0.7 convert_element_type.13
  6.4 0.3 copy-done.1
  6.7 0.7 convert_element_type.14
  7.5 0.0 copy-done.2
  7.5 0.1 fusion
  7.5 0.8 pad_maximum_fusion.refs_3_
  8.4 296.2 %decoder_step.1 = (f32[2,16,2432]{2,1,0:T(8,128)}, f32[2,16,4096]{2,1,0:T(8,128)}, f32[2,64,1024]{2,1,0:T(8,128)}, bf16[2,32,1024]{2,1,0:T(8,128)(2,1)}, bf16[2,32,1024]{2,1,0:T(8,128)(2,1)}) custom-call(bf16[2,16,2432]{2,1,0:T(8,128)(2,1)} %copy-done.6, bf16[2,16,4096]{2,1,0:T(8,128)(2,1)} %bitcast.30, bf16[2,64,1024]{2,1,0:T(8,128)(2,1)} %bitcast.31, ...), custom_call_target="tpu_custom_call" | custom-call | tf_op jit(solution)/shard_map/decoder_step/pallas_call | solution.py:701
  304.6 1.5 slice_reduce_fusion
  306.1 1.3 fusion.2
  307.5 1.7 fusion.1
  309.2 1.6 copy.40
  310.7 0.7 copy.41
  311.4 0.8 copy.42
  312.2 0.4 copy-done.4
  312.6 0.8 copy.43
  (19 shorter events, 0.1 us)
Async XLA Ops:
  0.6 5.0 %copy-start = (f32[32,4096]{1,0:T(8,128)S(1)}, f32[32,4096]{1,0:T(8,128)}, u32[]{:S(2)}) copy-start(f32[32,4096]{1,0:T(8,128)} %param.20) | copy-start | bytes 1572868
  5.5 1.2 copy-start.1
  5.6 1.8 copy-start.6
  5.6 1.8 copy-start.3
  6.4 1.1 copy-start.2
  304.6 6.1 %copy-start.7 = (bf16[2,32,1024]{2,1,0:T(8,128)(2,1)S(1)}, bf16[2,32,1024]{2,1,0:T(8,128)(2,1)}, u32[]{:S(2)}) copy-start(bf16[2,32,1024]{2,1,0:T(8,128)(2,1)} %get-tuple-element.16) | copy-start | bytes 393220
  304.6 6.8 %copy-start.5 = (f32[2,16,4096]{2,1,0:T(8,128)S(1)}, f32[2,16,4096]{2,1,0:T(8,128)}, u32[]{:S(2)}) copy-start(f32[2,16,4096]{2,1,0:T(8,128)} %get-tuple-element.18) | copy-start | bytes 1572868
  311.4 1.2 copy-start.4

commit v3 on v2

--- a/solution.py
+++ b/solution.py
@@ -107,6 +107,10 @@
     return lax.dot_general(left, right, (((0,), (0,)), ((), ())), preferred_element_type=F32)
 
 
+def dot_w(weight, value):
+    return jnp.transpose(dot(weight, jnp.transpose(value)))
+
+
 def rms_factor(values):
     return lax.rsqrt(jnp.mean(values * values, axis=-1, keepdims=True) + NORM_EPS)
 
@@ -139,15 +143,27 @@
         b.gains[:, start * 256 : (start + 1) * 256] = jnp.transpose(block)[0:8]
 
 
-def forward_layer(b, m):
-    pad = pad_column(b.act, m)
+def transpose_down(b):
+    @pl.loop(0, 4)
+    def _(n):
+        b.g2[:, :, :, :, :, tile(n, D)] = jnp.transpose(b.w3[n].reshape(D, D)).reshape(4, 4, 2, 2, 16, D)
+
+
+def transpose_up(b):
+    @pl.loop(0, 4)
+    def _(n):
+        b.g3[n] = jnp.transpose(b.w2[:, :, :, :, :, tile(n, D)].reshape(D, D)).reshape(4, 2, 2, 64, D)
+
+
+def forward_qkv(b, m):
     hidden = b.hb[m].astype(F32)
     b.xa[m] = (hidden * rms_factor(hidden) * b.gains[0:1, :]).astype(BF)
 
-    @pl.loop(0, (D + 2 * HD) // 256)
-    def _(n):
-        b.qkv[m, :, tile(n, 256)] = dot(b.xa[m], b.w1[:, :, :, :, :, tile(n, 256)].reshape(D, 256)).astype(BF)
-
+    wide = D + 2 * HD
+    b.qkv[m] = dot(b.xa[m], b.w1[:, :, :, :, :, 0:wide].reshape(D, wide)).astype(BF)
+
+
+def forward_attention(b, m):
     length = b.act[m, SEQ : SEQ + 1, 0:1].astype(F32)
     rows = lax.broadcasted_iota(jnp.int32, (SEQ, SEQ), 0)
     columns = lax.broadcasted_iota(jnp.int32, (SEQ, SEQ), 1)
@@ -161,40 +177,43 @@
     b.probs[m] = probs
     b.mixed[m] = heads_across(dot(probs.astype(BF), values_all)).astype(BF)
 
-    @pl.loop(0, D // 256)
-    def _(n):
-        w = b.w1[:, :, :, :, :, pl.ds(pl.multiple_of(W1 - D + n * 256, HD), 256)].reshape(D, 256)
-        b.after[m, :, tile(n, 256)] = b.hb[m, :, tile(n, 256)].astype(F32) + pad * dot(b.mixed[m], w)
+
+def forward_out(b, m):
+    pad = pad_column(b.act, m)
+
+    w = b.w1[:, :, :, :, :, W1 - D :].reshape(D, D)
+    b.after[m] = b.hb[m].astype(F32) + pad * dot(b.mixed[m], w)
 
     after = b.after[m]
     b.xf[m] = (after * rms_factor(after) * b.gains[1:2, :]).astype(BF)
 
-    @pl.loop(0, FF // 512)
-    def _(n):
-        a = dot(b.xf[m], b.w2[:, :, :, :, :, tile(n, 512)].reshape(D, 512))
-        sigmoid = 1.0 / (1.0 + jnp.exp(-a))
-        b.u[m, :, tile(n, 512)] = (a * sigmoid).astype(BF)
-        b.dp[m, :, tile(n, 512)] = (sigmoid * (1.0 + a * (1.0 - sigmoid))).astype(BF)
-
-    @pl.loop(0, D // 256)
-    def _(n):
-        w = b.w3[:, :, :, :, :, tile(n, 256)].reshape(FF, 256)
-        b.ho[m, :, tile(n, 256)] = (b.after[m, :, tile(n, 256)] + pad * dot(b.u[m], w)).astype(BF)
-
-
-def backward_ffn(b, m):
+
+def forward_up(b, m):
+    a = dot(b.xf[m], b.w2[...].reshape(D, FF))
+    sigmoid = 1.0 / (1.0 + jnp.exp(-a))
+    b.u[m] = (a * sigmoid).astype(BF)
+    b.dp[m] = (sigmoid * (1.0 + a * (1.0 - sigmoid))).astype(BF)
+
+
+def forward_down(b, m):
+    pad = pad_column(b.act, m)
+
+    b.ho[m] = (b.after[m] + pad * dot(b.u[m], b.w3[...].reshape(FF, D))).astype(BF)
+
+
+def backward_act(b, m):
     pad = pad_column(b.act, m)
     b.gf[m] = (b.gb[m].astype(F32) * pad).astype(BF)
 
-    @pl.loop(0, 16)
-    def _(n):
-        w = b.w3[n // 4, n % 4].reshape(256, D)
-        b.dp[m, :, tile(n, 256)] = (dot_nt(b.gf[m], w) * b.dp[m, :, tile(n, 256)].astype(F32)).astype(BF)
-
-    @pl.loop(0, 4)
-    def _(n):
-        b.dx[:, tile(n, 256)] = dot_nt(b.dp[m], b.w2[n].reshape(256, FF))
-
+    b.dp[m] = (dot(b.gf[m], b.g2[...].reshape(D, FF)) * b.dp[m].astype(F32)).astype(BF)
+
+
+def backward_up(b, m):
+    b.dx[...] = dot(b.dp[m], b.g3[...].reshape(FF, D))
+
+
+def backward_ffn_norm(b, m):
+    pad = pad_column(b.act, m)
     after = b.after[m]
     factor = rms_factor(after)
     normed = after * factor
@@ -205,13 +224,12 @@
     b.ga[m] = (d_r * pad).astype(BF)
 
 
+def backward_out(b, m):
+    b.do[...] = dot_w(b.w1[:, :, :, :, :, W1 - D :].reshape(D, D), b.ga[m]).astype(BF)
+
+
 def backward_attention(b, m):
     scale = HD ** (-0.5)
-
-    @pl.loop(0, 4)
-    def _(n):
-        b.do[:, tile(n, 256)] = dot_nt(b.ga[m], b.w1[n, :, :, :, :, W1 - D :].reshape(256, D)).astype(BF)
-
     d_mixed = heads_down(b.do[...])
     keys_all = b.qkv[m, :, D : D + HD]
     values_all = b.qkv[m, :, D + HD : D + 2 * HD]
@@ -222,11 +240,13 @@
     b.dqkv[m, :, 0:D] = heads_across(dot(d_s, keys_all) * scale).astype(BF)
     b.dqkv[m, :, D : D + HD] = (dot_tn(d_s, heads_down(b.qkv[m, :, 0:D])) * scale).astype(BF)
 
-    @pl.loop(0, 4)
-    def _(n):
-        w = b.w1[n, :, :, :, :, 0 : D + 2 * HD].reshape(256, D + 2 * HD)
-        b.dx[:, tile(n, 256)] = dot_nt(b.dqkv[m], w)
-
+
+def backward_qkv(b, m):
+    wide = D + 2 * HD
+    b.dx[...] = dot_w(b.w1[:, :, :, :, :, 0:wide].reshape(D, wide), b.dqkv[m])
+
+
+def backward_in(b, m):
     hidden = b.hb[m].astype(F32)
     factor = rms_factor(hidden)
     normed = hidden * factor
@@ -240,35 +260,40 @@
 
 
 def grads_down(b):
-    @pl.loop(0, 16)
-    def _(n):
-        left = b.u[:, :, tile(n, 256)].reshape(MICRO * SEQ, 256)
-        b.g3[n // 4, n % 4] = dot_tn(left, b.gf[...].reshape(MICRO * SEQ, D)).astype(BF).reshape(2, 2, 64, D)
+    left = b.u[...].reshape(MICRO * SEQ, FF)
+    b.g3[...] = dot_tn(left, b.gf[...].reshape(MICRO * SEQ, D)).astype(BF).reshape(4, 4, 2, 2, 64, D)
 
 
 def grads_up(b):
-    @pl.loop(0, 16)
-    def _(n):
-        left = b.xf[:, :, tile(n // 4, 256)].reshape(MICRO * SEQ, 256)
-        right = b.dp[:, :, tile(n % 4, D)].reshape(MICRO * SEQ, D)
-        b.g2[n // 4, :, :, :, :, tile(n % 4, D)] = dot_tn(left, right).astype(BF).reshape(4, 2, 2, 16, D)
+    right = b.dp[...].reshape(MICRO * SEQ, FF)
+    b.g2[...] = dot_tn(b.xf[...].reshape(MICRO * SEQ, D), right).astype(BF).reshape(4, 4, 2, 2, 16, FF)
 
 
 def grads_first(b):
     wide = D + 2 * HD
 
-    @pl.loop(0, 4)
-    def _(n):
-        left = b.xa[:, :, tile(n, 256)].reshape(MICRO * SEQ, 256)
-        b.g1[n, :, :, :, :, 0:wide] = dot_tn(left, b.dqkv[...].reshape(MICRO * SEQ, wide)).astype(BF).reshape(4, 2, 2, 16, wide)
-        left = b.mixed[:, :, tile(n, 256)].reshape(MICRO * SEQ, 256)
-        b.g1[n, :, :, :, :, W1 - D :] = dot_tn(left, b.ga[...].reshape(MICRO * SEQ, D)).astype(BF).reshape(4, 2, 2, 16, D)
+    left = b.xa[...].reshape(MICRO * SEQ, D)
+    b.g1[:, :, :, :, :, 0:wide] = dot_tn(left, b.dqkv[...].reshape(MICRO * SEQ, wide)).astype(BF).reshape(4, 4, 2, 2, 16, wide)
+    left = b.mixed[...].reshape(MICRO * SEQ, D)
+    b.g1[:, :, :, :, :, W1 - D :] = dot_tn(left, b.ga[...].reshape(MICRO * SEQ, D)).astype(BF).reshape(4, 4, 2, 2, 16, D)
 
     lines = [jnp.sum(b.gain_sums[k, 0] + b.gain_sums[k, 1], axis=0, keepdims=True) for k in range(2)]
     sums = jnp.concatenate(lines + [jnp.zeros((HD - 2, D), F32)], axis=0)
     for n in range(4):
         block = jnp.transpose(sums[:, n * 256 : (n + 1) * 256]).astype(BF)
         b.g1[n, :, :, :, :, D + 2 * HD : D + 3 * HD] = block.reshape(4, 2, 2, 16, HD)
+
+
+FORWARD = (forward_qkv, forward_attention, forward_out, forward_up, forward_down)
+BACKWARD = (
+    backward_act,
+    backward_up,
+    backward_ffn_norm,
+    backward_out,
+    backward_attention,
+    backward_qkv,
+    backward_in,
+)
 
 
 N_GATHER = 12
@@ -657,25 +682,45 @@
         at = which * MICRO + m
         return remote(b.ho.at[m], dst.at[m], (sem.relay_send.at[at], sem.relay_recv.at[at]), role.dev(there, y, z, c))
 
+    early = jnp.logical_or(jnp.logical_not(first), c == 1)
+
+    @pl.when(early)
+    def _():
+        transpose_down(b)
+
+    @pl.when(jnp.logical_not(first))
+    def _():
+        transpose_up(b)
+
     final_rows = Rows(role, 0, b.ho, final_out, sem)
     start_rows = Rows(role, 1, b.ho, start_out, sem)
 
     @pl.loop(0, MICRO)
     def _(m):
         pl.when(jnp.logical_not(first))(lambda: relay(0, m).wait_recv())
-        forward_layer(b, m)
+        for phase in FORWARD:
+            phase(b, m)
         pl.when(jnp.logical_not(last))(lambda: relay(0, m).start())
         final_rows.start(m)
+
+    @pl.when(jnp.logical_not(early))
+    def _():
+        transpose_down(b)
+
+    @pl.when(first)
+    def _():
+        transpose_up(b)
 
     scatter = Scatter(role, (b.g1, b.g2, b.g3), (b.w1, b.w2, b.w3), swaps, (o1, o2, o3), sem, free)
 
     @pl.loop(0, MICRO)
     def _(m):
         pl.when(jnp.logical_not(last))(lambda: relay(1, m).wait_recv())
-        backward_ffn(b, m)
+        for phase in BACKWARD[:-1]:
+            phase(b, m)
         pl.when(jnp.logical_not(last))(lambda: relay(0, m).wait_send())
         final_rows.sent(m)
-        backward_attention(b, m)
+        BACKWARD[-1](b, m)
         pl.when(jnp.logical_not(first))(lambda: relay(1, m).start())
         start_rows.start(m)
 

time: 314 us -> 265 us (0.84)
  Pallas kernels: 296 us -> 247 us
    pallas_call x1, Pallas kernels: 296 us -> 247 us  [decoder(): pl.pallas_call(decoder_kernel, out_shape=[jax.ShapeDtypeStruct(shape, F32...]
where the time goes in v3:
time: 265 us; the launch traced here: 264 us
  Pallas kernels  247 us (93%)
  local copies, waits for them, and re-layouts  9.4 us (4%)
  other arithmetic  7.04 us (3%)
    pallas_call x1, Pallas kernels, decoder(): pl.pallas_call(decoder_kernel, out_shape=[jax.ShapeDtypeStruct(shape, F32...  247 us

profile of v3, /device:TPU:1, one launch (start us, length us, event | category | flops | bytes accessed | tf_op | source)
XLA Modules:
  0.0 264.2 jit_solution(10457011765802577422)
XLA Ops:
  0.7 0.7 convert_bitcast_fusion
  1.4 0.7 convert_bitcast_fusion.1
  2.1 0.1 copy.31
  2.2 0.7 convert.29
  2.9 0.7 convert.30
  3.6 0.1 broadcast_in_dim.15
  3.7 0.9 convert.28
  4.6 0.9 convert.33
  5.6 0.0 copy-start.3
  5.6 0.7 convert_element_type.13
  6.4 0.3 copy-done.1
  6.7 0.7 convert_element_type.14
  7.5 0.0 copy-done.2
  7.5 0.1 fusion
  7.5 0.8 pad_maximum_fusion.refs_3_
  8.4 247.0 %decoder_step.1 = (f32[2,16,2432]{2,1,0:T(8,128)}, f32[2,16,4096]{2,1,0:T(8,128)}, f32[2,64,1024]{2,1,0:T(8,128)}, bf16[2,32,1024]{2,1,0:T(8,128)(2,1)}, bf16[2,32,1024]{2,1,0:T(8,128)(2,1)}) custom-call(bf16[2,16,2432]{2,1,0:T(8,128)(2,1)} %copy-done.6, bf16[2,16,4096]{2,1,0:T(8,128)(2,1)} %bitcast.30, bf16[2,64,1024]{2,1,0:T(8,128)(2,1)} %bitcast.31, ...), custom_call_target="tpu_custom_call" | custom-call | tf_op jit(solution)/shard_map/decoder_step/pallas_call | solution.py:746
  255.4 1.5 slice_reduce_fusion
  256.9 1.3 fusion.2
  258.3 1.7 fusion.1
  259.9 1.6 copy.40
  261.5 0.7 copy.41
  262.2 0.8 copy.42
  263.0 0.4 copy-done.4
  263.4 0.8 copy.43
  (19 shorter events, 0.1 us)
Async XLA Ops:
  0.6 5.0 %copy-start = (f32[32,4096]{1,0:T(8,128)S(1)}, f32[32,4096]{1,0:T(8,128)}, u32[]{:S(2)}) copy-start(f32[32,4096]{1,0:T(8,128)} %param.20) | copy-start | bytes 1572868
  5.5 1.2 copy-start.1
  5.6 1.8 copy-start.6
  5.6 1.8 copy-start.3
  6.4 1.1 copy-start.2
  255.4 6.1 %copy-start.7 = (bf16[2,32,1024]{2,1,0:T(8,128)(2,1)S(1)}, bf16[2,32,1024]{2,1,0:T(8,128)(2,1)}, u32[]{:S(2)}) copy-start(bf16[2,32,1024]{2,1,0:T(8,128)(2,1)} %get-tuple-element.16) | copy-start | bytes 393220
  255.4 6.8 %copy-start.5 = (f32[2,16,4096]{2,1,0:T(8,128)S(1)}, f32[2,16,4096]{2,1,0:T(8,128)}, u32[]{:S(2)}) copy-start(f32[2,16,4096]{2,1,0:T(8,128)} %get-tuple-element.18) | copy-start | bytes 1572868
  262.2 1.2 copy-start.4

commit v4 on v3

--- a/solution.py
+++ b/solution.py
@@ -55,10 +55,8 @@
 
 
 def greet(devices):
-    barrier = pltpu.get_barrier_semaphore()
     for device in devices:
-        pl.semaphore_signal(barrier, inc=1, device_id=device, device_id_type=MESH)
-    pl.semaphore_wait(barrier, len(devices))
+        pl.semaphore_signal(pltpu.get_barrier_semaphore(), inc=1, device_id=device, device_id_type=MESH)
 
 
 class Bufs:
@@ -72,7 +70,9 @@
     ("g1", (4, 4, 2, 2, 16, W1), BF),
     ("g2", (4, 4, 2, 2, 16, FF), BF),
     ("g3", (4, 4, 2, 2, 64, D), BF),
-    ("act", (MICRO, SEQ + 16, D), BF),
+    ("act", (MICRO, SEQ, D), BF),
+    ("lens", (MICRO, 16, HD), BF),
+    ("lens_own", (MICRO, 16, HD), BF),
     ("hb", (MICRO, SEQ, D), BF),
     ("gb", (MICRO, SEQ, D), BF),
     ("ho", (MICRO, SEQ, D), BF),
@@ -131,8 +131,8 @@
     return jnp.concatenate([value[h * SEQ : (h + 1) * SEQ] for h in range(HEADS)], axis=1)
 
 
-def pad_column(act, m):
-    length = act[m, SEQ : SEQ + 1, 0:1].astype(F32)
+def pad_column(lens, m):
+    length = lens[m, 0:1, 0:1].astype(F32)
     positions = lax.broadcasted_iota(jnp.int32, (SEQ, 1), 0).astype(F32)
     return jnp.where(positions < length, 1.0, 0.0)
 
@@ -164,7 +164,7 @@
 
 
 def forward_attention(b, m):
-    length = b.act[m, SEQ : SEQ + 1, 0:1].astype(F32)
+    length = b.lens[m, 0:1, 0:1].astype(F32)
     rows = lax.broadcasted_iota(jnp.int32, (SEQ, SEQ), 0)
     columns = lax.broadcasted_iota(jnp.int32, (SEQ, SEQ), 1)
     allowed = jnp.logical_and(columns <= rows, columns.astype(F32) < length)
@@ -179,7 +179,7 @@
 
 
 def forward_out(b, m):
-    pad = pad_column(b.act, m)
+    pad = pad_column(b.lens, m)
 
     w = b.w1[:, :, :, :, :, W1 - D :].reshape(D, D)
     b.after[m] = b.hb[m].astype(F32) + pad * dot(b.mixed[m], w)
@@ -196,13 +196,13 @@
 
 
 def forward_down(b, m):
-    pad = pad_column(b.act, m)
+    pad = pad_column(b.lens, m)
 
     b.ho[m] = (b.after[m] + pad * dot(b.u[m], b.w3[...].reshape(FF, D))).astype(BF)
 
 
 def backward_act(b, m):
-    pad = pad_column(b.act, m)
+    pad = pad_column(b.lens, m)
     b.gf[m] = (b.gb[m].astype(F32) * pad).astype(BF)
 
     b.dp[m] = (dot(b.gf[m], b.g2[...].reshape(D, FF)) * b.dp[m].astype(F32)).astype(BF)
@@ -213,7 +213,7 @@
 
 
 def backward_ffn_norm(b, m):
-    pad = pad_column(b.act, m)
+    pad = pad_column(b.lens, m)
     after = b.after[m]
     factor = rms_factor(after)
     normed = after * factor
@@ -298,20 +298,15 @@
 
 N_GATHER = 12
 N_SCATTER = 9
-GATHER_CUTS = ((0, 1), (1, 2), (2, 2))
-SCATTER_CUTS = ((2, 2), (1, 2), (0, 1))
-STEPS = 5
-WIDTHS = (W1, FF, D)
+GATHER_CHUNKS = ((0, 0, 1280), (0, 1280, 1152), (1, 0, 2048), (1, 2048, 2048), (2, 0, 512), (2, 512, 512))
+SCATTER_CHUNKS = ((1, 0, 2048), (1, 2048, 2048), (2, 0, 512), (2, 512, 512), (0, 0, 1280), (0, 1280, 1152))
+RING = 3
 SEMAPHORES = (
-    ("ag_send", STEPS * 2 * N_GATHER),
-    ("ag_recv", STEPS * 2 * N_GATHER),
-    ("ag_swap_send", STEPS + 1),
-    ("ag_swap_recv", STEPS + 1),
-    ("ag_local", STEPS + 1),
-    ("rs_send", STEPS * 2 * N_SCATTER),
-    ("rs_recv", STEPS * 2 * N_SCATTER),
-    ("rs_swap_send", STEPS * 2),
-    ("rs_swap_recv", STEPS * 2),
+    ("send", RING * 2 * N_GATHER),
+    ("recv", 6 * 2 * N_GATHER),
+    ("swap_send", 12),
+    ("swap_recv", 12),
+    ("local", 9),
     ("relay_send", 2 * MICRO),
     ("relay_recv", 2 * MICRO),
     ("row_send", 2 * MICRO * LAYERS),
@@ -320,124 +315,133 @@
 )
 
 
-def cut(cuts):
-    made = []
-    for which, count in cuts:
-        wide = WIDTHS[which] // count
-        for at in range(count):
-            made.append((which, at * wide, wide))
-    return made
-
-
 def near_far(chunk, part):
     which, start, wide = chunk
     near = (wide // HD + 1) // 2 * HD
     return pl.ds(start, near) if part == 0 else pl.ds(start + near, wide - near)
 
 
-def gather_weights(role, shards, fulls, act_in, b, sem):
-    y, z, c = role.y, role.z, role.c
-    place = (y, z)
-    chunks = cut(GATHER_CUTS)
-    count = len(chunks)
-
-    def own_copies(step, owner):
-        which, start, wide = chunks[step]
-        src = shards[which].at[:, :, pl.ds(start, wide)]
-        dst = fulls[which].at[y, z, owner, :, :, pl.ds(start, wide)]
+class Gather:
+    ARRIVE = ((), (0, 1), (2, 3), (4, 5), (6, 7), (8, 9, 10, 11))
+    LEAVE = ((0, 1), (2, 3), (4, 5, 8), (6, 7, 9, 10), (11,), ())
+
+    def __init__(self, role, shards, fulls, acts, act, lens_own, lens, sem):
+        self.role, self.shards, self.fulls, self.sem = role, shards, fulls, sem
+        self.acts, self.act, self.lens_own, self.lens = acts, act, lens_own, lens
+        self.chunks = GATHER_CHUNKS
+
+    def own_copies(self, step, owner):
+        role = self.role
+        which, start, wide = self.chunks[step]
+        src = self.shards[which].at[:, :, pl.ds(start, wide)]
+        dst = self.fulls[which].at[role.y, role.z, owner, :, :, pl.ds(start, wide)]
         return (
-            remote(src, dst, (sem.ag_swap_send.at[step], sem.ag_swap_recv.at[step]), role.swap()),
-            pltpu.make_async_copy(src, dst, sem.ag_local.at[step]),
+            remote(src, dst, (self.sem.swap_send.at[step], self.sem.swap_recv.at[step]), role.swap()),
+            pltpu.make_async_copy(src, dst, self.sem.local.at[step]),
         )
 
-    act_far = remote(act_in, b.act, (sem.ag_swap_send.at[count], sem.ag_swap_recv.at[count]), role.swap())
-    act_near = pltpu.make_async_copy(act_in, b.act, sem.ag_local.at[count])
-
-    @pl.when(role.native)
-    def _():
-        for step in range(count):
-            own_copies(step, c)[1].start()
-        act_near.start()
-
-    @pl.when(jnp.logical_not(role.native))
-    def _():
-        for step in range(count):
-            own_copies(step, 1 - c)[0].start()
-        act_far.start()
-
-    def piece(step, half, first, second, part=None):
-        which, start, wide = chunks[step]
-        cols = pl.ds(start, wide) if part is None else near_far(chunks[step], part)
-        index = (first, second) if half == 0 else (second, first)
-        return fulls[which].at[index[0], index[1], c, half, :, cols]
-
-    def hop(step, half, number):
+    def extra_copies(self):
+        made = []
+        for at, (src, dst) in enumerate(((self.acts[0], self.act), (self.acts[1], self.act), (self.lens_own, self.lens))):
+            at = len(self.chunks) + (0 if at < 2 else 1)
+            made.append(
+                (
+                    remote(src, dst, (self.sem.swap_send.at[at], self.sem.swap_recv.at[at]), self.role.swap()),
+                    pltpu.make_async_copy(src, dst, self.sem.local.at[at]),
+                )
+            )
+        return made
+
+    def open(self):
+        role = self.role
+
+        def each(kind, act):
+            for step in range(len(self.chunks)):
+                getattr(self.own_copies(step, role.c if kind else 1 - role.c)[kind], act)()
+            extra = self.extra_copies()
+            pl.when(role.x < 2)(lambda: getattr(extra[0][kind], act)())
+            pl.when(role.x >= 2)(lambda: getattr(extra[1][kind], act)())
+            getattr(extra[2][kind], act)()
+
+        pl.when(role.native)(lambda: each(1, "start"))
+        pl.when(jnp.logical_not(role.native))(lambda: each(0, "start"))
+
+    def close_extra(self):
+        role = self.role
+        extra = self.extra_copies()
+        for kind, native in ((1, role.native), (0, jnp.logical_not(role.native))):
+
+            @pl.when(native)
+            def _():
+                extra[0][kind].wait()
+                extra[2][kind].wait()
+
+    def hop(self, step, half, number):
+        role = self.role
+        which, start, wide = self.chunks[step]
+        place = (role.y, role.z)
         one, two = half, 1 - half
         p, s = place[one], place[two]
         nxt, prv = (p + 1) % 4, (p + 3) % 4
         snx, spv, sop = (s + 1) % 4, (s + 3) % 4, (s + 2) % 4
         every, low, high = slice(None), pl.ds(0, 2), pl.ds(2, 2)
-        first, second, part, device = (
-            (p, s, None, role.along(one, 1)),
-            (p, s, None, role.along(one, -1)),
-            (prv, s, 0, role.along(one, 1)),
-            (nxt, s, 1, role.along(one, -1)),
-            (every, s, None, role.along(two, 1)),
-            (every, s, None, role.along(two, -1)),
-            (low, spv, None, role.along(two, 1)),
-            (high, snx, None, role.along(two, -1)),
-            (every, s, None, role.partner()),
-            (every, spv, None, role.partner()),
-            (every, snx, None, role.partner()),
-            (every, sop, None, role.partner()),
+        first, second, part, axis = (
+            (p, s, None, one),
+            (p, s, None, one),
+            (prv, s, 0, one),
+            (nxt, s, 1, one),
+            (every, s, None, two),
+            (every, s, None, two),
+            (low, spv, None, two),
+            (high, snx, None, two),
+            (every, s, None, None),
+            (every, spv, None, None),
+            (every, snx, None, None),
+            (every, sop, None, None),
         )[number]
-        view = piece(step, half, first, second, part)
-        at = (step * 2 + half) * N_GATHER + number
-        return remote(view, view, (sem.ag_send.at[at], sem.ag_recv.at[at]), device)
-
-    arrive = ((), (0, 1), (2, 3), (4, 5), (6, 7))
-    leave = ((0, 1), (2, 3), (4, 5, 8), (6, 7, 9, 10), (11,))
-    for tick in range(count + 4):
-        for level in range(5):
-            step = tick - level
-            if not 0 <= step < count:
-                continue
-            if level == 0:
-
-                @pl.when(role.native)
-                def _():
-                    own_copies(step, c)[1].wait()
-
-                @pl.when(jnp.logical_not(role.native))
-                def _():
-                    own_copies(step, 1 - c)[0].wait()
-
+        device = role.partner() if axis is None else role.along(axis, 1 if number % 2 == 0 else -1)
+        cols = pl.ds(start, wide) if part is None else near_far(self.chunks[step], part)
+        index = (first, second) if half == 0 else (second, first)
+        view = self.fulls[which].at[index[0], index[1], role.c, half, :, cols]
+        at = (step % RING * 2 + half) * N_GATHER + number
+        to = (step * 2 + half) * N_GATHER + number
+        return remote(view, view, (self.sem.send.at[at], self.sem.recv.at[to]), device)
+
+    def level(self, step, number):
+        role = self.role
+        if number == 0:
+            pl.when(role.native)(lambda: self.own_copies(step, role.c)[1].wait())
+            pl.when(jnp.logical_not(role.native))(lambda: self.own_copies(step, 1 - role.c)[0].wait())
+        for half in (0, 1):
+            for hop in self.ARRIVE[number]:
+                self.hop(step, half, hop).wait_recv()
+            for hop in self.LEAVE[number]:
+                if step >= RING:
+                    self.hop(step - RING, half, hop).wait_send()
+                self.hop(step, half, hop).start()
+
+    def run(self, hooks):
+        count = len(self.chunks)
+        for tick in range(count + 5):
+            for number in range(6):
+                step = tick - number
+                if 0 <= step < count:
+                    self.level(step, number)
+            if tick - 5 in hooks:
+                hooks[tick - 5]()
+
+    def finish(self):
+        for step in range(len(self.chunks) - RING, len(self.chunks)):
             for half in (0, 1):
-                for number in arrive[level]:
-                    hop(step, half, number).wait_recv()
-                for number in leave[level]:
-                    hop(step, half, number).start()
-    for step in range(count):
-        for half in (0, 1):
-            for number in (8, 9, 10, 11):
-                hop(step, half, number).wait_recv()
-            for number in range(N_GATHER):
-                hop(step, half, number).wait_send()
-
-    @pl.when(role.native)
-    def _():
-        act_near.wait()
-
-    @pl.when(jnp.logical_not(role.native))
-    def _():
-        act_far.wait()
+                for number in range(N_GATHER):
+                    self.hop(step, half, number).wait_send()
 
 
 class Scatter:
     def __init__(self, role, grads, works, swaps, outs, sem, free):
         self.role, self.grads, self.works, self.swaps, self.outs = role, grads, works, swaps, outs
         self.sem, self.free = sem, free
-        self.chunks = cut(SCATTER_CUTS)
+        self.chunks = SCATTER_CHUNKS
         self.peers = [role.along(0, 1), role.along(0, -1), role.along(1, 1), role.along(1, -1), role.partner()]
 
     def say_free(self, which):
@@ -453,11 +457,12 @@
 
     def core_copy(self, step):
         which = self.chunks[step][0]
-        at = step * 2 * N_SCATTER
+        at = step % RING * 2 * N_SCATTER
+        to = step * 2 * N_SCATTER
         return remote(
             self.grads[which].at[:, :, 1 - self.role.c, :, :, self.cols(step)],
             self.works[which].at[:, :, 0, :, :, self.cols(step)],
-            (self.sem.rs_send.at[at], self.sem.rs_recv.at[at]),
+            (self.sem.send.at[at], self.sem.recv.at[to]),
             self.role.partner(),
         )
 
@@ -489,11 +494,12 @@
             ((p, spv, None), (3, 3, None)),
         )[number]
         axis = one if number < 4 else two
-        at = (step * 2 + half) * N_SCATTER + 1 + number
+        at = (step % RING * 2 + half) * N_SCATTER + 1 + number
+        to = (step * 2 + half) * N_SCATTER + 1 + number
         return remote(
             self.piece(step, half, *src),
             self.spot(step, half, *dst),
-            (self.sem.rs_send.at[at], self.sem.rs_recv.at[at]),
+            (self.sem.send.at[at], self.sem.recv.at[to]),
             role.along(axis, 1 if number % 2 == 0 else -1),
         )
 
@@ -503,7 +509,7 @@
         return remote(
             self.grads[which].at[self.role.y, self.role.z, self.role.c, half, :, self.cols(step)],
             self.swaps[which].at[half, :, self.cols(step)],
-            (self.sem.rs_swap_send.at[at], self.sem.rs_swap_recv.at[at]),
+            (self.sem.swap_send.at[at], self.sem.swap_recv.at[at]),
             self.role.swap(),
         )
 
@@ -562,37 +568,51 @@
                 self.swapped(step, half).start()
 
         if number < 4:
-            self.hop(step, half, 2 * number).start()
-            self.hop(step, half, 2 * number + 1).start()
-
-    def run(self):
+            for hop in (2 * number, 2 * number + 1):
+                if step >= RING:
+                    self.hop(step - RING, half, hop).wait_send()
+                self.hop(step, half, hop).start()
+
+    def core(self, which):
+        self.wait_free(which)
+        for step, chunk in enumerate(self.chunks):
+            if chunk[0] == which:
+                if step >= RING:
+                    self.core_copy(step - RING).wait_send()
+                self.core_copy(step).start()
+
+    def enter(self, step):
+        self.add_core(step)
+        for half in (0, 1):
+            self.level(step, half, 0)
+
+    def leave(self, step):
+        which = self.chunks[step][0]
+
+        @pl.when(jnp.logical_not(self.role.native))
+        def _():
+            for half in (0, 1):
+                self.swapped(step, half).wait()
+                self.outs[which][half, :, self.cols(step)] = self.swaps[which][half, :, self.cols(step)].astype(F32)
+
+    def run(self, start):
         count = len(self.chunks)
-        for step in range(count):
-            which = self.chunks[step][0]
-            if step == 0 or self.chunks[step - 1][0] != which:
-                self.wait_free(which)
-            self.core_copy(step).start()
-        for tick in range(count + 4):
-            for number in range(4, -1, -1):
-                step = tick - number
-                if 0 <= step < count:
-                    if number == 0:
-                        self.add_core(step)
+        for tick in range(count + 5):
+            for number in range(1, 6):
+                step = tick - number + 1
+                if number == 1 and start <= tick + 1 < count:
+                    self.enter(tick + 1)
+                if not 0 <= step < count:
+                    continue
+                if number == 5:
+                    self.leave(step)
+                else:
                     for half in (0, 1):
                         self.level(step, half, number)
 
     def finish(self):
-        role = self.role
-
-        @pl.when(jnp.logical_not(role.native))
-        def _():
-            for step in range(len(self.chunks)):
-                which = self.chunks[step][0]
-                for half in (0, 1):
-                    self.swapped(step, half).wait()
-                    self.outs[which][half, :, self.cols(step)] = self.swaps[which][half, :, self.cols(step)].astype(F32)
-
-        for step in range(len(self.chunks)):
+        count = len(self.chunks)
+        for step in range(count - RING, count):
             self.core_copy(step).wait_send()
             for half in (0, 1):
                 for number in range(8):
@@ -644,144 +664,275 @@
             self.copies(m)[0][1].wait_recv()
 
 
+def load_shards(role, weights, lengths, stages, b, sem):
+    w_query, w_key, w_value, w_out, attn_gain, ffn_gain, w_up, w_down = weights
+    rows = D // 32
+    pairs = [
+        (w_query, b.dx.at[0:rows]),
+        (w_out, b.dx.at[rows : 2 * rows]),
+        (w_key, b.probs.at[0, 0:rows]),
+        (w_value, b.probs.at[0, rows : 2 * rows]),
+    ]
+    pairs += [(w_up.at[:, pl.ds(n * D, D)], b.after.at[1, n * rows : (n + 1) * rows]) for n in range(4)]
+    pairs += [(w_down, b.after.at[0])]
+    copies = [pltpu.make_async_copy(src, dst, sem.local.at[at]) for at, (src, dst) in enumerate(pairs)]
+    for copy in copies:
+        copy.start()
+
+    for copy in copies:
+        copy.wait()
+    first, second, third = stages
+    down = lax.broadcasted_iota(jnp.int32, (rows, rows), 0)
+    across = lax.broadcasted_iota(jnp.int32, (rows, rows), 1)
+
+    def column(gain):
+        line = jnp.broadcast_to(gain[...].reshape(1, rows), (rows, rows))
+        return jnp.sum(jnp.where(down == across, line, 0.0), axis=1, keepdims=True)
+
+    lane = lax.broadcasted_iota(jnp.int32, (rows, HD), 1)
+    gains = jnp.where(lane == 0, column(attn_gain), jnp.where(lane == 1, column(ffn_gain), 0.0))
+    first[:, :, 0:D] = b.dx[0:rows].astype(BF).reshape(2, 16, D)
+    first[:, :, D : D + HD] = b.probs[0, 0:rows].astype(BF).reshape(2, 16, HD)
+    first[:, :, D + HD : D + 2 * HD] = b.probs[0, rows : 2 * rows].astype(BF).reshape(2, 16, HD)
+    first[:, :, D + 2 * HD : D + 3 * HD] = gains.astype(BF).reshape(2, 16, HD)
+    first[:, :, W1 - D :] = b.dx[rows : 2 * rows].astype(BF).reshape(2, 16, D)
+    for n in range(4):
+        second[:, :, n * D : (n + 1) * D] = b.after[1, n * rows : (n + 1) * rows].astype(BF).reshape(2, 16, D)
+    third[...] = b.after[0].astype(BF).reshape(2, 64, D)
+    for m in range(MICRO):
+        b.lens_own[m] = jnp.broadcast_to(lengths[m : m + 1, 0:1].astype(F32), (16, HD)).astype(BF)
+
+
 def decoder_kernel(*refs):
-    names = [name for name, _, _ in SCRATCH]
-    s1, s2, s3, act_in, o1, o2, o3, final_out, start_out = refs[:9]
+    inputs, cotangent, lengths = refs[:3]
+    weights = refs[3:11]
+    o1, o2, o3, final_out, start_out = refs[11:16]
     b, sem = Bufs(), Bufs()
-    rest = list(refs[9:])
-    for name in names:
+    rest = list(refs[16:])
+    for name, _, _ in SCRATCH:
         setattr(b, name, rest.pop(0))
     swaps = [rest.pop(0) for _ in range(3)]
     for name, _ in SEMAPHORES:
         setattr(sem, name, rest.pop(0))
     free = rest.pop(0)
+    turn = rest.pop(0)
 
     role = Role()
     x, y, z, c = role.x, role.y, role.z, role.c
+    first, last = x == 0, x == LAYERS - 1
+    later, before_last = jnp.logical_not(first), jnp.logical_not(last)
     peers = [role.along(0, 1), role.along(0, -1), role.along(1, 1), role.along(1, -1)]
     for away in range(4):
         for other in range(2):
             if (away, other) != (0, 0):
                 peers.append(role.dev((x + away) % 4, y, z, (c + other) % 2))
     greet(peers)
-
-    gather_weights(role, (s1, s2, s3), (b.w1, b.w2, b.w3), act_in, b, sem)
-    read_gains(b)
-    first, last = x == 0, x == LAYERS - 1
-
-    @pl.when(first)
-    def _():
-        b.hb[...] = b.act[:, 0:SEQ]
-
-    @pl.when(last)
-    def _():
-        b.gb[...] = b.act[:, 0:SEQ]
+    load_shards(role, weights, lengths, swaps, b, sem)
+    pl.semaphore_wait(pltpu.get_barrier_semaphore(), len(peers))
+
+    gather = Gather(role, swaps, (b.w1, b.w2, b.w3), (inputs, cotangent), b.act, b.lens_own, b.lens, sem)
+
+    def with_first():
+        gather.close_extra()
+        read_gains(b)
+
+        @pl.when(last)
+        def _():
+            b.gb[...] = b.act[...]
+
+        @pl.when(first)
+        def _():
+            b.hb[...] = b.act[...]
+
+            @pl.loop(0, MICRO)
+            def _(m):
+                for phase in FORWARD[:3]:
+                    phase(b, m)
+
+    def with_up():
+        @pl.when(first)
+        def _():
+            @pl.loop(0, MICRO)
+            def _(m):
+                forward_up(b, m)
+
+    gather.open()
+    ends = [max(step for step, chunk in enumerate(gather.chunks) if chunk[0] == which) for which in range(3)]
+    gather.run({ends[0]: with_first, ends[1]: with_up})
+    gather.finish()
 
     def relay(which, m):
         dst, there = ((b.hb, (x + 1) % 4), (b.gb, (x + 3) % 4))[which]
         at = which * MICRO + m
         return remote(b.ho.at[m], dst.at[m], (sem.relay_send.at[at], sem.relay_recv.at[at]), role.dev(there, y, z, c))
 
-    early = jnp.logical_or(jnp.logical_not(first), c == 1)
-
-    @pl.when(early)
+    final_rows = Rows(role, 0, b.ho, final_out, sem)
+    start_rows = Rows(role, 1, b.ho, start_out, sem)
+
+    @pl.when(jnp.logical_or(later, c == 1))
     def _():
         transpose_down(b)
 
-    @pl.when(jnp.logical_not(first))
-    def _():
-        transpose_up(b)
-
-    final_rows = Rows(role, 0, b.ho, final_out, sem)
-    start_rows = Rows(role, 1, b.ho, start_out, sem)
+    pl.when(later)(lambda: transpose_up(b))
 
     @pl.loop(0, MICRO)
     def _(m):
-        pl.when(jnp.logical_not(first))(lambda: relay(0, m).wait_recv())
-        for phase in FORWARD:
-            phase(b, m)
-        pl.when(jnp.logical_not(last))(lambda: relay(0, m).start())
+        @pl.when(later)
+        def _():
+            relay(0, m).wait_recv()
+            for phase in FORWARD[:4]:
+                phase(b, m)
+
+        forward_down(b, m)
+
+        @pl.when(jnp.logical_and(first, jnp.logical_and(m == MICRO - 1, c == 1)))
+        def _():
+            pl.semaphore_wait(turn, 1)
+
+        pl.when(before_last)(lambda: relay(0, m).start())
         final_rows.start(m)
 
-    @pl.when(jnp.logical_not(early))
+        @pl.when(jnp.logical_and(first, m == 0))
+        def _():
+            pl.when(c == 0)(lambda: transpose_down(b))
+            transpose_up(b)
+
+    @pl.when(jnp.logical_and(first, c == 0))
     def _():
-        transpose_down(b)
-
-    @pl.when(first)
-    def _():
-        transpose_up(b)
+        relay(0, MICRO - 1).wait_send()
+        pl.semaphore_signal(turn, inc=1, device_id=role.partner(), device_id_type=MESH)
 
     scatter = Scatter(role, (b.g1, b.g2, b.g3), (b.w1, b.w2, b.w3), swaps, (o1, o2, o3), sem, free)
+    scatter.say_free(1)
+    scatter.say_free(2)
+
+    def up_made():
+        grads_up(b)
+        scatter.core(1)
+
+    def down_made():
+        grads_down(b)
+        scatter.core(2)
 
     @pl.loop(0, MICRO)
     def _(m):
-        pl.when(jnp.logical_not(last))(lambda: relay(1, m).wait_recv())
-        for phase in BACKWARD[:-1]:
-            phase(b, m)
-        pl.when(jnp.logical_not(last))(lambda: relay(0, m).wait_send())
+        ahead = jnp.logical_and(first, m == MICRO - 1)
+        pl.when(before_last)(lambda: relay(1, m).wait_recv())
+        backward_act(b, m)
+        pl.when(ahead)(up_made)
+        backward_up(b, m)
+        pl.when(ahead)(down_made)
+        backward_ffn_norm(b, m)
+        backward_out(b, m)
+        backward_attention(b, m)
+        backward_qkv(b, m)
+        held = jnp.logical_and(before_last, jnp.logical_or(later, jnp.logical_or(c == 1, m < MICRO - 1)))
+        pl.when(held)(lambda: relay(0, m).wait_send())
         final_rows.sent(m)
-        BACKWARD[-1](b, m)
-        pl.when(jnp.logical_not(first))(lambda: relay(1, m).start())
+        backward_in(b, m)
+        pl.when(later)(lambda: relay(1, m).start())
         start_rows.start(m)
 
-    for which in (2, 1, 0):
-        scatter.say_free(which)
-    grads_down(b)
-    grads_up(b)
+    scatter.say_free(0)
+
+    @pl.when(later)
+    def _():
+        up_made()
+        down_made()
+
+    scatter.enter(0)
+    scatter.enter(1)
     grads_first(b)
-    scatter.run()
+    scatter.core(0)
+    scatter.run(2)
     scatter.finish()
     for m in range(MICRO):
-        pl.when(jnp.logical_not(first))(lambda: relay(1, m).wait_send())
+        pl.when(later)(lambda: relay(1, m).wait_send())
         start_rows.sent(m)
         final_rows.arrived(m)
         start_rows.arrived(m)
 
 
-def decoder(s1, s2, s3, act):
-    hbm = pl.BlockSpec(memory_space=pl.ANY)
-    vmem = pl.BlockSpec(memory_space=pltpu.VMEM)
-    shapes = [s.shape for s in (s1, s2, s3)]
+HBM = pl.BlockSpec(memory_space=pl.ANY)
+IN_VMEM = pl.BlockSpec(memory_space=pltpu.VMEM)
+
+
+def decoder(inputs, cotangent, lengths, weights):
+    shapes = [(2, 16, W1), (2, 16, FF), (2, 64, D)]
     rows = SEQ // LAYERS
     return pl.pallas_call(
         decoder_kernel,
         out_shape=[jax.ShapeDtypeStruct(shape, F32) for shape in shapes]
         + [jax.ShapeDtypeStruct((MICRO, rows, D), BF)] * 2,
-        in_specs=[hbm] * 4,
-        out_specs=[vmem] * 3 + [hbm] * 2,
+        in_specs=[HBM, HBM, IN_VMEM] + [HBM] * 4 + [IN_VMEM] * 2 + [HBM] * 2,
+        out_specs=[IN_VMEM] * 3 + [HBM] * 2,
         scratch_shapes=[pltpu.VMEM(shape, dtype) for _, shape, dtype in SCRATCH]
         + [pltpu.VMEM(shape, BF) for shape in shapes]
         + [pltpu.SemaphoreType.DMA((count,)) for _, count in SEMAPHORES]
-        + [pltpu.SemaphoreType.REGULAR((3,))],
+        + [pltpu.SemaphoreType.REGULAR((3,)), pltpu.SemaphoreType.REGULAR],
         compiler_params=pltpu.CompilerParams(collective_id=0, has_side_effects=True, vmem_limit_bytes=63 << 20),
         name="decoder_step",
-    )(s1, s2, s3, act)
+    )(inputs, cotangent, lengths, *weights)
+
+
+def deliver_kernel(o1, o2, o3, final_in, start_in, *rest):
+    final_out, start_out, attn_gain, w_query, w_key, w_value, w_out, ffn_gain, w_up, w_down = rest
+    final_out[...] = final_in[...]
+    start_out[...] = start_in[...]
+    w_query[...] = o1[:, :, 0:D]
+    w_key[...] = o1[:, :, D : D + HD]
+    w_value[...] = o1[:, :, D + HD : D + 2 * HD]
+    w_out[...] = o1[:, :, W1 - D :]
+    w_up[...] = o2[...]
+    w_down[...] = o3[...]
+    rows = D // 32
+    down = lax.broadcasted_iota(jnp.int32, (rows, rows), 0)
+    across = lax.broadcasted_iota(jnp.int32, (rows, rows), 1)
+    columns = o1[:, :, D + 2 * HD : D + 3 * HD].reshape(rows, HD)
+    for at, gain in ((0, attn_gain), (1, ffn_gain)):
+        wide = jnp.broadcast_to(columns[:, at : at + 1], (rows, rows))
+        gain[...] = jnp.sum(jnp.where(down == across, wide, 0.0), axis=0)
+
+
+def deliver(o1, o2, o3, final_rows, start_rows):
+    shapes = [
+        (final_rows.shape, BF),
+        (start_rows.shape, BF),
+        ((32,), F32),
+        ((2, 16, D), F32),
+        ((2, 16, HD), F32),
+        ((2, 16, HD), F32),
+        ((2, 16, D), F32),
+        ((32,), F32),
+        ((2, 16, FF), F32),
+        ((2, 64, D), F32),
+    ]
+    return pl.pallas_call(
+        deliver_kernel,
+        out_shape=[jax.ShapeDtypeStruct(shape, dtype) for shape, dtype in shapes],
+        in_specs=[IN_VMEM] * 5,
+        out_specs=[IN_VMEM] * len(shapes),
+        name="deliver",
+    )(o1, o2, o3, final_rows, start_rows)
 
 
 def body(
     inputs, cotangent, lengths, attn_gain, w_query, w_key, w_value, w_out, ffn_gain, w_up, w_down
 ):
-    role = Role()
-    gains = jnp.pad(jnp.stack([attn_gain, ffn_gain], axis=1), ((0, 0), (0, HD - 2)))
-    first = jnp.concatenate([w_query, w_key, w_value, gains, w_out], axis=1).astype(BF).reshape(2, 16, W1)
-    second = w_up.astype(BF).reshape(2, 16, FF)
-    third = w_down.astype(BF).reshape(2, 64, D)
-    rows = jnp.where(role.x < 2, inputs[:, 0], cotangent[:, 0])
-    lengths_rows = jnp.broadcast_to(lengths.astype(BF)[:, :, None], (MICRO, 16, D))
-    act = jnp.concatenate([rows, lengths_rows], axis=1)
-    o1, o2, o3, final_rows, input_rows = decoder(first, second, third, act)
-    o1 = o1.reshape(32, W1)
+    weights = (w_query, w_key, w_value, w_out, attn_gain, ffn_gain, w_up, w_down)
+    made = deliver(*decoder(inputs[:, 0], cotangent[:, 0], lengths, weights))
+    final_rows, start_rows, g_attn, g_query, g_key, g_value, g_out, g_ffn, g_up, g_down = made
     return (
         final_rows[:, None],
-        input_rows[:, None],
-        o1[:, D + 2 * HD],
-        o1[:, :D],
-        o1[:, D : D + HD],
-        o1[:, D + HD : D + 2 * HD],
-        o1[:, W1 - D :],
-        o1[:, D + 2 * HD + 1],
-        o2.reshape(32, FF),
-        o3.reshape(128, D),
+        start_rows[:, None],
+        g_attn,
+        g_query.reshape(32, D),
+        g_key.reshape(32, HD),
+        g_value.reshape(32, HD),
+        g_out.reshape(32, D),
+        g_ffn,
+        g_up.reshape(32, FF),
+        g_down.reshape(128, D),
     )
 
 

time: 265 us -> 240 us (0.906)
  Pallas kernels: 247 us -> 236 us
  local copies, waits for them, and re-layouts: 9.4 us -> 1.3 us
  other arithmetic: 7.04 us -> 0 us
    pallas_call x1, Pallas kernels: 247 us -> 234 us  [decoder(): pl.pallas_call(decoder_kernel, out_shape=[jax.ShapeDtypeStruct(shape, F32...]
    slice x3 -> x0, local copies, waits for them, and re-layouts: 4.53 us -> none  [the longest x1 1.68 us: body(): o1[:, W1 - D:]]
    another operation x6 -> x0, other arithmetic: 3.95 us -> none
    unnamed x25 -> x3, local copies, waits for them, and re-layouts: 4.78 us -> 1.3 us
where the time goes in v4:
time: 240 us; the launch traced here: 238 us
  Pallas kernels  236 us (98%)
    pallas_call x1, Pallas kernels, decoder(): pl.pallas_call(decoder_kernel, out_shape=[jax.ShapeDtypeStruct(shape, F32...  234 us

profile of v4, /device:TPU:1, one launch (start us, length us, event | category | flops | bytes accessed | tf_op | source)
XLA Modules:
  0.0 238.2 jit_solution(9999450543201825158)
XLA Ops:
  0.6 0.0 copy-start
  0.7 0.6 copy-done
  1.3 0.6 copy.21.refs_2_
  1.9 233.7 %decoder_step.1 = (f32[2,16,2432]{2,1,0:T(8,128)}, f32[2,16,4096]{2,1,0:T(8,128)}, f32[2,64,1024]{2,1,0:T(8,128)}, bf16[2,32,1024]{2,1,0:T(8,128)(2,1)}, bf16[2,32,1024]{2,1,0:T(8,128)(2,1)}) custom-call(bf16[2,128,1024]{2,1,0:T(8,128)(2,1)} %bitcast.14, bf16[2,128,1024]{2,1,0:T(8,128)(2,1)} %bitcast.15, s32[2,1]{1,0:T(2,128)} %copy.21.refs_2_, ...), custom_call_target="tpu_custom_call" | custom-call | tf_op jit(solution)/shard_map/decoder_step/pallas_call | solution.py:863
  235.7 2.5 %deliver.1 = (bf16[2,32,1024]{2,1,0:T(8,128)(2,1)}, bf16[2,32,1024]{2,1,0:T(8,128)(2,1)}, f32[32]{0:T(128)}, f32[2,16,1024]{2,1,0:T(8,128)}, f32[2,16,128]{2,1,0...) custom-call(f32[2,16,2432]{2,1,0:T(8,128)} %get-tuple-element.25.o1,, ...), custom_call_target="tpu_custom_call" | custom-call | tf_op jit(solution)/shard_map/deliver/pallas_call | solution.py:910
Async XLA Ops:
  0.6 0.7 copy-start

commit v5 on v4

--- a/solution.py
+++ b/solution.py
@@ -190,9 +190,10 @@
 
 def forward_up(b, m):
     a = dot(b.xf[m], b.w2[...].reshape(D, FF))
-    sigmoid = 1.0 / (1.0 + jnp.exp(-a))
-    b.u[m] = (a * sigmoid).astype(BF)
-    b.dp[m] = (sigmoid * (1.0 + a * (1.0 - sigmoid))).astype(BF)
+    sigmoid = 0.5 + 0.5 * jnp.tanh(0.5 * a)
+    u = a * sigmoid
+    b.u[m] = u.astype(BF)
+    b.dp[m] = (sigmoid + u * (1.0 - sigmoid)).astype(BF)
 
 
 def forward_down(b, m):
@@ -264,9 +265,11 @@
     b.g3[...] = dot_tn(left, b.gf[...].reshape(MICRO * SEQ, D)).astype(BF).reshape(4, 4, 2, 2, 64, D)
 
 
-def grads_up(b):
-    right = b.dp[...].reshape(MICRO * SEQ, FF)
-    b.g2[...] = dot_tn(b.xf[...].reshape(MICRO * SEQ, D), right).astype(BF).reshape(4, 4, 2, 2, 16, FF)
+def grads_up(b, start, end):
+    wide = end - start
+    right = b.dp[:, :, start:end].reshape(MICRO * SEQ, wide)
+    made = dot_tn(b.xf[...].reshape(MICRO * SEQ, D), right).astype(BF)
+    b.g2[:, :, :, :, :, start:end] = made.reshape(4, 4, 2, 2, 16, wide)
 
 
 def grads_first(b):
@@ -299,13 +302,21 @@
 N_GATHER = 12
 N_SCATTER = 9
 GATHER_CHUNKS = ((0, 0, 1280), (0, 1280, 1152), (1, 0, 2048), (1, 2048, 2048), (2, 0, 512), (2, 512, 512))
-SCATTER_CHUNKS = ((1, 0, 2048), (1, 2048, 2048), (2, 0, 512), (2, 512, 512), (0, 0, 1280), (0, 1280, 1152))
+SCATTER_CHUNKS = (
+    (1, 0, 1024),
+    (1, 1024, 1536),
+    (1, 2560, 1536),
+    (2, 0, 512),
+    (2, 512, 512),
+    (0, 0, 1664),
+    (0, 1664, 768),
+)
 RING = 3
 SEMAPHORES = (
     ("send", RING * 2 * N_GATHER),
     ("recv", 6 * 2 * N_GATHER),
-    ("swap_send", 12),
-    ("swap_recv", 12),
+    ("swap_send", 14),
+    ("swap_recv", 14),
     ("local", 9),
     ("relay_send", 2 * MICRO),
     ("relay_recv", 2 * MICRO),
@@ -424,9 +435,9 @@
         count = len(self.chunks)
         for tick in range(count + 5):
             for number in range(6):
-                step = tick - number
-                if 0 <= step < count:
-                    self.level(step, number)
+                for step in (2 * tick, 2 * tick + 1) if number == 0 else (tick - number,):
+                    if 0 <= step < count:
+                        self.level(step, number)
             if tick - 5 in hooks:
                 hooks[tick - 5]()
 
@@ -573,18 +584,23 @@
                     self.hop(step - RING, half, hop).wait_send()
                 self.hop(step, half, hop).start()
 
-    def core(self, which):
-        self.wait_free(which)
-        for step, chunk in enumerate(self.chunks):
-            if chunk[0] == which:
-                if step >= RING:
-                    self.core_copy(step - RING).wait_send()
-                self.core_copy(step).start()
+    def core(self, *steps):
+        for step in steps:
+            which = self.chunks[step][0]
+            if step == 0 or self.chunks[step - 1][0] != which:
+                self.wait_free(which)
+            if step >= RING:
+                self.core_copy(step - RING).wait_send()
+            self.core_copy(step).start()
 
     def enter(self, step):
         self.add_core(step)
         for half in (0, 1):
             self.level(step, half, 0)
+
+    def pair(self, step, number):
+        for half in (0, 1):
+            self.level(step, half, number)
 
     def leave(self, step):
         which = self.chunks[step][0]
@@ -595,20 +611,19 @@
                 self.swapped(step, half).wait()
                 self.outs[which][half, :, self.cols(step)] = self.swaps[which][half, :, self.cols(step)].astype(F32)
 
-    def run(self, start):
+    def run(self):
         count = len(self.chunks)
-        for tick in range(count + 5):
+        for tick in range(2, count + 5):
             for number in range(1, 6):
                 step = tick - number + 1
-                if number == 1 and start <= tick + 1 < count:
+                if number == 1 and tick + 1 < count:
                     self.enter(tick + 1)
                 if not 0 <= step < count:
                     continue
                 if number == 5:
                     self.leave(step)
                 else:
-                    for half in (0, 1):
-                        self.level(step, half, number)
+                    self.pair(step, number)
 
     def finish(self):
         count = len(self.chunks)
@@ -715,7 +730,6 @@
     for name, _ in SEMAPHORES:
         setattr(sem, name, rest.pop(0))
     free = rest.pop(0)
-    turn = rest.pop(0)
 
     role = Role()
     x, y, z, c = role.x, role.y, role.z, role.c
@@ -769,11 +783,10 @@
     final_rows = Rows(role, 0, b.ho, final_out, sem)
     start_rows = Rows(role, 1, b.ho, start_out, sem)
 
-    @pl.when(jnp.logical_or(later, c == 1))
+    @pl.when(later)
     def _():
         transpose_down(b)
-
-    pl.when(later)(lambda: transpose_up(b))
+        transpose_up(b)
 
     @pl.loop(0, MICRO)
     def _(m):
@@ -785,34 +798,27 @@
 
         forward_down(b, m)
 
-        @pl.when(jnp.logical_and(first, jnp.logical_and(m == MICRO - 1, c == 1)))
-        def _():
-            pl.semaphore_wait(turn, 1)
-
         pl.when(before_last)(lambda: relay(0, m).start())
         final_rows.start(m)
 
-        @pl.when(jnp.logical_and(first, m == 0))
-        def _():
-            pl.when(c == 0)(lambda: transpose_down(b))
-            transpose_up(b)
-
-    @pl.when(jnp.logical_and(first, c == 0))
+    @pl.when(first)
     def _():
-        relay(0, MICRO - 1).wait_send()
-        pl.semaphore_signal(turn, inc=1, device_id=role.partner(), device_id_type=MESH)
+        transpose_down(b)
+        transpose_up(b)
 
     scatter = Scatter(role, (b.g1, b.g2, b.g3), (b.w1, b.w2, b.w3), swaps, (o1, o2, o3), sem, free)
     scatter.say_free(1)
     scatter.say_free(2)
 
     def up_made():
-        grads_up(b)
-        scatter.core(1)
+        grads_up(b, 0, D)
+        scatter.core(0)
+        grads_up(b, D, FF)
+        scatter.core(1, 2)
 
     def down_made():
         grads_down(b)
-        scatter.core(2)
+        scatter.core(3, 4)
 
     @pl.loop(0, MICRO)
     def _(m):
@@ -821,13 +827,19 @@
         backward_act(b, m)
         pl.when(ahead)(up_made)
         backward_up(b, m)
-        pl.when(ahead)(down_made)
+
+        @pl.when(ahead)
+        def _():
+            scatter.enter(0)
+            down_made()
+            scatter.enter(1)
+            scatter.pair(0, 1)
+
         backward_ffn_norm(b, m)
         backward_out(b, m)
         backward_attention(b, m)
         backward_qkv(b, m)
-        held = jnp.logical_and(before_last, jnp.logical_or(later, jnp.logical_or(c == 1, m < MICRO - 1)))
-        pl.when(held)(lambda: relay(0, m).wait_send())
+        pl.when(before_last)(lambda: relay(0, m).wait_send())
         final_rows.sent(m)
         backward_in(b, m)
         pl.when(later)(lambda: relay(1, m).start())
@@ -838,13 +850,17 @@
     @pl.when(later)
     def _():
         up_made()
+        scatter.enter(0)
         down_made()
-
-    scatter.enter(0)
-    scatter.enter(1)
+        scatter.enter(1)
+        scatter.pair(0, 1)
+
+    scatter.enter(2)
+    scatter.pair(1, 1)
     grads_first(b)
-    scatter.core(0)
-    scatter.run(2)
+    scatter.core(5, 6)
+    scatter.pair(0, 2)
+    scatter.run()
     scatter.finish()
     for m in range(MICRO):
         pl.when(later)(lambda: relay(1, m).wait_send())
@@ -869,7 +885,7 @@
         scratch_shapes=[pltpu.VMEM(shape, dtype) for _, shape, dtype in SCRATCH]
         + [pltpu.VMEM(shape, BF) for shape in shapes]
         + [pltpu.SemaphoreType.DMA((count,)) for _, count in SEMAPHORES]
-        + [pltpu.SemaphoreType.REGULAR((3,)), pltpu.SemaphoreType.REGULAR],
+        + [pltpu.SemaphoreType.REGULAR((3,))],
         compiler_params=pltpu.CompilerParams(collective_id=0, has_side_effects=True, vmem_limit_bytes=63 << 20),
         name="decoder_step",
     )(inputs, cotangent, lengths, *weights)

time: 240 us -> 229 us (0.954)
  Pallas kernels: 236 us -> 226 us
    pallas_call x1, Pallas kernels: 234 us -> 224 us  [decoder(): pl.pallas_call(decoder_kernel, out_shape=[jax.ShapeDtypeStruct(shape, F32...]
where the time goes in v5:
time: 229 us; the launch traced here: 228 us
  Pallas kernels  226 us (99%)
    pallas_call x1, Pallas kernels, decoder(): pl.pallas_call(decoder_kernel, out_shape=[jax.ShapeDtypeStruct(shape, F32...  224 us

profile of v5, /device:TPU:1, one launch (start us, length us, event | category | flops | bytes accessed | tf_op | source)
XLA Modules:
  0.0 228.1 jit_solution(18239755624117231306)
XLA Ops:
  0.6 0.0 copy-start
  0.7 0.6 copy-done
  1.3 0.6 copy.21.refs_2_
  1.9 223.7 %decoder_step.1 = (f32[2,16,2432]{2,1,0:T(8,128)}, f32[2,16,4096]{2,1,0:T(8,128)}, f32[2,64,1024]{2,1,0:T(8,128)}, bf16[2,32,1024]{2,1,0:T(8,128)(2,1)}, bf16[2,32,1024]{2,1,0:T(8,128)(2,1)}) custom-call(bf16[2,128,1024]{2,1,0:T(8,128)(2,1)} %bitcast.14, bf16[2,128,1024]{2,1,0:T(8,128)(2,1)} %bitcast.15, s32[2,1]{1,0:T(2,128)} %copy.21.refs_2_, ...), custom_call_target="tpu_custom_call" | custom-call | tf_op jit(solution)/shard_map/decoder_step/pallas_call | solution.py:879
  225.6 2.5 %deliver.1 = (bf16[2,32,1024]{2,1,0:T(8,128)(2,1)}, bf16[2,32,1024]{2,1,0:T(8,128)(2,1)}, f32[32]{0:T(128)}, f32[2,16,1024]{2,1,0:T(8,128)}, f32[2,16,128]{2,1,0...) custom-call(f32[2,16,2432]{2,1,0:T(8,128)} %get-tuple-element.25.o1,, ...), custom_call_target="tpu_custom_call" | custom-call | tf_op jit(solution)/shard_map/deliver/pallas_call | solution.py:926
Async XLA Ops:
  0.6 0.7 copy-start

commit v6 on v5

--- a/solution.py
+++ b/solution.py
@@ -788,27 +788,7 @@
         transpose_down(b)
         transpose_up(b)
 
-    @pl.loop(0, MICRO)
-    def _(m):
-        @pl.when(later)
-        def _():
-            relay(0, m).wait_recv()
-            for phase in FORWARD[:4]:
-                phase(b, m)
-
-        forward_down(b, m)
-
-        pl.when(before_last)(lambda: relay(0, m).start())
-        final_rows.start(m)
-
-    @pl.when(first)
-    def _():
-        transpose_down(b)
-        transpose_up(b)
-
     scatter = Scatter(role, (b.g1, b.g2, b.g3), (b.w1, b.w2, b.w3), swaps, (o1, o2, o3), sem, free)
-    scatter.say_free(1)
-    scatter.say_free(2)
 
     def up_made():
         grads_up(b, 0, D)
@@ -820,9 +800,18 @@
         grads_down(b)
         scatter.core(3, 4)
 
-    @pl.loop(0, MICRO)
-    def _(m):
-        ahead = jnp.logical_and(first, m == MICRO - 1)
+    def forward(m):
+        @pl.when(later)
+        def _():
+            relay(0, m).wait_recv()
+            for phase in FORWARD[:4]:
+                phase(b, m)
+
+        forward_down(b, m)
+        pl.when(before_last)(lambda: relay(0, m).start())
+        final_rows.start(m)
+
+    def backward(m, ahead):
         pl.when(before_last)(lambda: relay(1, m).wait_recv())
         backward_act(b, m)
         pl.when(ahead)(up_made)
@@ -844,6 +833,24 @@
         backward_in(b, m)
         pl.when(later)(lambda: relay(1, m).start())
         start_rows.start(m)
+
+    @pl.loop(0, 2 * MICRO)
+    def _(turn):
+        m = jnp.where(last, turn // 2, turn % 2)
+        onward = jnp.where(last, turn % 2, turn // 2) == 0
+
+        @pl.when(jnp.logical_and(first, turn == MICRO))
+        def _():
+            transpose_down(b)
+            transpose_up(b)
+
+        @pl.when(turn == 2 * MICRO - 1)
+        def _():
+            scatter.say_free(1)
+            scatter.say_free(2)
+
+        pl.when(onward)(lambda: forward(m))
+        pl.when(jnp.logical_not(onward))(lambda: backward(m, jnp.logical_and(first, turn == 2 * MICRO - 1)))
 
     scatter.say_free(0)
 

time: 229 us -> 225 us (0.983)
  Pallas kernels: 226 us -> 223 us
    pallas_call x1, Pallas kernels: 224 us -> 220 us  [decoder(): pl.pallas_call(decoder_kernel, out_shape=[jax.ShapeDtypeStruct(shape, F32...]
where the time goes in v6:
time: 225 us
  Pallas kernels  223 us (99%)
    pallas_call x1, Pallas kernels, decoder(): pl.pallas_call(decoder_kernel, out_shape=[jax.ShapeDtypeStruct(shape, F32...  220 us

profile of v6, /device:TPU:1, one launch (start us, length us, event | category | flops | bytes accessed | tf_op | source)
XLA Modules:
  0.0 224.8 jit_solution(963075598538624554)
XLA Ops:
  0.6 0.0 copy-start
  0.7 0.6 copy-done
  1.3 0.6 copy.21.refs_2_
  1.9 220.3 %decoder_step.1 = (f32[2,16,2432]{2,1,0:T(8,128)}, f32[2,16,4096]{2,1,0:T(8,128)}, f32[2,64,1024]{2,1,0:T(8,128)}, bf16[2,32,1024]{2,1,0:T(8,128)(2,1)}, bf16[2,32,1024]{2,1,0:T(8,128)(2,1)}) custom-call(bf16[2,128,1024]{2,1,0:T(8,128)(2,1)} %bitcast.14, bf16[2,128,1024]{2,1,0:T(8,128)(2,1)} %bitcast.15, s32[2,1]{1,0:T(2,128)} %copy.21.refs_2_, ...), custom_call_target="tpu_custom_call" | custom-call | tf_op jit(solution)/shard_map/decoder_step/pallas_call | solution.py:886
  222.3 2.5 %deliver.1 = (bf16[2,32,1024]{2,1,0:T(8,128)(2,1)}, bf16[2,32,1024]{2,1,0:T(8,128)(2,1)}, f32[32]{0:T(128)}, f32[2,16,1024]{2,1,0:T(8,128)}, f32[2,16,128]{2,1,0...) custom-call(f32[2,16,2432]{2,1,0:T(8,128)} %get-tuple-element.25.o1,, ...), custom_call_target="tpu_custom_call" | custom-call | tf_op jit(solution)/shard_map/deliver/pallas_call | solution.py:933
Async XLA Ops:
  0.6 0.7 copy-start
